TPU v7x, 32 devices: a whole 2x2x4 slice. The times are simulated.
32 devices in a mesh: dp: 8 (over z, y), mp: 4 (over x, core).
Axes of the slice: x: 2, y: 2, z: 4, core: 2. Of those that a mesh axis runs over, the one named last changes fastest.
Arguments:
- residual: bfloat16 [16384, 768], P('dp', 'mp'), may hold values from -6 to 6, as said below
- lengths: int32 [8, 4], P('dp'), may hold values from 0 to 2048, as said below
- gain_one: float32 [768], P('mp'), may hold values from 0.5 to 1.5
- input_weight: bfloat16 [3, 768, 768], P(None, None, 'mp'), may hold values from -0.21875 to 0.21875
- input_bias: float32 [2, 768], P(None, 'mp'), may hold values from -1.8 to 1.8
- output_weight: bfloat16 [768, 768], P('mp'), may hold values from -2.5 to 2.5
- output_bias: float32 [768], P('mp'), may hold values from -1.8 to 1.8
- gain_two: float32 [768], P('mp'), may hold values from 0.5 to 1.5
- expand_weight: bfloat16 [768, 3072], P(None, 'mp'), may hold values from -0.21875 to 0.21875
- expand_bias: float32 [3072], P('mp'), may hold values from -1.8 to 1.8
- reduce_weight: bfloat16 [3072, 768], P('mp'), may hold values from -0.109375 to 0.109375
- reduce_bias: float32 [768], P('mp'), may hold values from -1.8 to 1.8
- cotangent: bfloat16 [16384, 768], P('dp', 'mp'), may hold values from -6 to 6
Outputs:
- residual_out: bfloat16 [16384, 768], P('dp', 'mp')
- residual_grad: bfloat16 [16384, 768], P('dp', 'mp')
- input_weight_grad: float32 [3, 768, 768], P(None, None, 'mp')
- input_bias_grad: float32 [2, 768], P(None, 'mp')
- output_weight_grad: float32 [768, 768], P('mp')
- output_bias_grad: float32 [768], P('mp')
- gain_one_grad: float32 [768], P('mp')
- gain_two_grad: float32 [768], P('mp')
- expand_weight_grad: float32 [768, 3072], P(None, 'mp')
- expand_bias_grad: float32 [3072], P('mp')
- reduce_weight_grad: float32 [3072, 768], P('mp')
- reduce_bias_grad: float32 [768], P('mp')
- residual_rms: float32 [], replicated
- live_count: int32 [], replicated
Inputs may be any that keep to these rules, and one draw needn't show every extreme that they name: Each row holds one group's sequence lengths by slot: first some of 2048, then some of 512, then zeros for unused slots; a row sums to at most 2048, and the first row holds a sequence of 2048. `residual`: column 767 is not read.
All inputs are finite; a program needn't handle non-finite values.
Results may differ from a plain program's by a relative error of at most 0.015.
Values may be sent and summed in bfloat16 or wider, within the bound.
A program may use at most 128 MiB of HBM per device.

v0:
```python
import jax
import jax.numpy as jnp
from jax import lax
from jax.sharding import PartitionSpec as P

D = 768
HEAD = 64
SHORT = 512
LONG = 2048


EPSILON = 1e-05
SCORE_SCALE = 0.125
NEGATIVE = -1e30


def smooth(inputs):
    return jax.nn.gelu(inputs, approximate=True)


def layout(width):
    columns = lax.axis_index("mp") * width + jnp.arange(width)
    return (columns < D - 1, columns == D - 1)


def segments(seq_lengths, row_count):
    seq_ends = jnp.cumsum(seq_lengths)
    positions = jnp.arange(row_count)
    segment = jnp.sum((positions[:, None] >= seq_ends[None, :]).astype(jnp.int32), axis=1)
    return (segment, positions < seq_ends[-1])


def window(row_start, row_count, segment, live_rows):
    key_start = jnp.clip(row_start + SHORT - LONG, 0, row_count - LONG)
    query_pos = row_start + jnp.arange(SHORT)
    key_pos = key_start + jnp.arange(LONG)
    query_seg = lax.dynamic_slice_in_dim(segment, row_start, SHORT)
    query_live = lax.dynamic_slice_in_dim(live_rows, row_start, SHORT)
    causal = key_pos[None, :] <= query_pos[:, None]
    allowed = (query_seg[:, None] == segment[None, :]) & causal & query_live[:, None]
    return (key_start, allowed | (key_pos[None, :] == query_pos[:, None]))


def column_sums(values):
    return lax.psum((jnp.sum(values, axis=1), jnp.sum(values * values, axis=1)), "mp")


def gather_normed(normed):
    return lax.all_gather(normed, "mp", axis=1, tiled=True)


def sum_branch(partial_rows, bias_vec):
    return (
        lax.psum_scatter(partial_rows, "mp", scatter_dimension=1, tiled=True) + bias_vec[None, :],
        None,
    )


def spread_grads(grad_rows):
    return lax.all_gather(grad_rows, "mp", axis=1, tiled=True)


def feature_sums(partial_rows):
    return lax.psum_scatter(
        partial_rows.astype(jnp.bfloat16), "mp", scatter_dimension=1, tiled=True
    ).astype(jnp.float32)


def normalize(values, row_total, row_squares, pad_mask, gain_vec):
    decompressed = jnp.where(pad_mask[None, :], -row_total[:, None], values)
    inverse = lax.rsqrt((row_squares + row_total * row_total) / D + EPSILON)
    return (decompressed, inverse, decompressed * inverse[:, None] * gain_vec[None, :])


def add_branch(values, branch, stored):
    kept = stored[None, :]
    row_mean = lax.psum(jnp.sum(branch, axis=1), "mp") / D
    result = values + jnp.where(kept, branch - row_mean[:, None], 0.0)
    new_total, new_squares = column_sums(result)
    return (result, new_total, new_squares)


def attend_forward(queries, key_rows, value_rows, segment, live_rows):
    row_count = queries.shape[0]

    def attend_block(block_index):
        row_start = block_index * SHORT
        key_start, allowed = window(row_start, row_count, segment, live_rows)
        query_block = lax.dynamic_slice_in_dim(queries, row_start, SHORT, 0)
        scores = (
            jnp.einsum("qhd,khd->hqk", query_block, key_rows, preferred_element_type=jnp.float32)
            * SCORE_SCALE
        )
        scores = jnp.where(allowed[None], scores, NEGATIVE)
        row_max = jnp.max(scores, axis=2, keepdims=True)
        weights = jnp.exp(scores - row_max)
        row_sum = jnp.sum(weights, axis=2, keepdims=True)
        attn_probs = (weights / row_sum).astype(jnp.bfloat16)
        result = jnp.einsum(
            "hqk,khd->qhd", attn_probs, value_rows, preferred_element_type=jnp.float32
        )
        return (result.astype(jnp.bfloat16), (row_max + jnp.log(row_sum))[:, :, 0])

    blocks, log_totals = lax.map(attend_block, jnp.arange(row_count // SHORT, dtype=jnp.int32))
    return (blocks.reshape(row_count, queries.shape[1], queries.shape[2]), log_totals)


def attend_backward(queries, key_rows, value_rows, grad_mixed, log_totals, segment, live_rows):
    row_count = queries.shape[0]

    def step(block_index, running):
        grad_queries, grad_keys, grad_values = running
        row_start = block_index * SHORT
        key_start, allowed = window(row_start, row_count, segment, live_rows)
        query_block = lax.dynamic_slice_in_dim(queries, row_start, SHORT, 0)
        grad_block = lax.dynamic_slice_in_dim(grad_mixed, row_start, SHORT, 0)
        scores = (
            jnp.einsum("qhd,khd->hqk", query_block, key_rows, preferred_element_type=jnp.float32)
            * SCORE_SCALE
        )
        scores = jnp.where(allowed[None], scores, NEGATIVE)
        attn_probs = jnp.exp(scores - log_totals[block_index][:, :, None])
        grad_probs = jnp.einsum(
            "qhd,khd->hqk", grad_block, value_rows, preferred_element_type=jnp.float32
        )
        centered = grad_probs - jnp.sum(attn_probs * grad_probs, axis=2, keepdims=True)
        grad_scores = (attn_probs * centered).astype(jnp.bfloat16)
        query_part = (
            jnp.einsum("hqk,khd->qhd", grad_scores, key_rows, preferred_element_type=jnp.float32)
            * SCORE_SCALE
        )
        key_part = (
            jnp.einsum("hqk,qhd->khd", grad_scores, query_block, preferred_element_type=jnp.float32)
            * SCORE_SCALE
        )
        value_part = jnp.einsum(
            "hqk,qhd->khd",
            attn_probs.astype(jnp.bfloat16),
            grad_block,
            preferred_element_type=jnp.float32,
        )
        grad_queries = lax.dynamic_update_slice_in_dim(grad_queries, query_part, row_start, 0)
        grad_keys = grad_keys + key_part
        grad_values = grad_values + value_part
        return (grad_queries, grad_keys, grad_values)

    empty = jnp.zeros(queries.shape, jnp.float32)
    return lax.fori_loop(0, row_count // SHORT, step, (empty, empty, empty))


def on_device(
    residual,
    lengths,
    gain_one,
    input_weight,
    input_bias,
    output_weight,
    output_bias,
    gain_two,
    expand_weight,
    expand_bias,
    reduce_weight,
    reduce_bias,
    cotangent,
):
    row_count, width = residual.shape
    heads_here = width // HEAD
    stored, pad_mask = layout(width)
    segment, live_rows = segments(lengths[0], row_count)
    live_count = lax.psum(jnp.sum(lengths), "dp")
    values = jnp.where(stored[None, :], residual.astype(jnp.float32), 0.0)
    row_total, row_squares = column_sums(values)
    full_one, inverse_one, normed_one = normalize(
        values, row_total, row_squares, pad_mask, gain_one
    )
    rows_one = gather_normed(normed_one.astype(jnp.bfloat16))
    projected = jnp.einsum(
        "td,cde->cte", rows_one, input_weight, preferred_element_type=jnp.float32
    )
    queries = (
        (projected[0] + input_bias[0][None, :])
        .astype(jnp.bfloat16)
        .reshape(row_count, heads_here, HEAD)
    )
    key_rows = projected[1].astype(jnp.bfloat16).reshape(row_count, heads_here, HEAD)
    value_rows = (
        (projected[2] + input_bias[1][None, :])
        .astype(jnp.bfloat16)
        .reshape(row_count, heads_here, HEAD)
    )
    mixed, log_totals = attend_forward(queries, key_rows, value_rows, segment, live_rows)
    mixed = mixed.reshape(row_count, width)
    branch_one, branch_one_total = sum_branch(
        jnp.dot(mixed, output_weight, preferred_element_type=jnp.float32), output_bias
    )
    values_one, total_one, squares_one = add_branch(values, branch_one, stored)
    full_two, inverse_two, normed_two = normalize(
        values_one, total_one, squares_one, pad_mask, gain_two
    )
    rows_two = gather_normed(normed_two.astype(jnp.bfloat16))
    hidden = (
        jnp.dot(rows_two, expand_weight, preferred_element_type=jnp.float32) + expand_bias[None, :]
    )
    active = smooth(hidden).astype(jnp.bfloat16)
    branch_two, branch_two_total = sum_branch(
        jnp.dot(active, reduce_weight, preferred_element_type=jnp.float32), reduce_bias
    )
    values_two, total_two, squares_two = add_branch(values_one, branch_two, stored)
    residual_out = values_two.astype(jnp.bfloat16)
    square_part = jnp.sum(jnp.where(live_rows, squares_two + total_two * total_two, 0.0))
    gradients = jnp.where(stored[None, :], cotangent.astype(jnp.float32), 0.0)
    grad_total = lax.psum(jnp.sum(gradients, axis=1), "mp")
    grad_branch_two = gradients - grad_total[:, None] / D
    reduce_bias_grad = jnp.sum(grad_branch_two, axis=0)
    rows_grad_two = spread_grads(grad_branch_two.astype(jnp.bfloat16))
    reduce_weight_grad = jnp.einsum(
        "tf,td->fd", active, rows_grad_two, preferred_element_type=jnp.float32
    )
    grad_active = jnp.einsum(
        "td,fd->tf", rows_grad_two, reduce_weight, preferred_element_type=jnp.float32
    )
    grad_hidden = jax.vjp(smooth, hidden)[1](grad_active)[0].astype(jnp.bfloat16)
    expand_bias_grad = jnp.sum(grad_hidden, axis=0, dtype=jnp.float32)
    expand_weight_grad = jnp.einsum(
        "td,tf->df", rows_two, grad_hidden, preferred_element_type=jnp.float32
    )
    grad_normed_two = feature_sums(
        jnp.einsum("tf,df->td", grad_hidden, expand_weight, preferred_element_type=jnp.float32)
    )
    gain_two_grad = jnp.sum(grad_normed_two * full_two * inverse_two[:, None], axis=0)
    scaled_two = grad_normed_two * gain_two[None, :]
    projected_two, scaled_total, pad_term = lax.psum(
        (
            jnp.sum(scaled_two * full_two, axis=1),
            jnp.sum(scaled_two, axis=1),
            jnp.sum(jnp.where(pad_mask[None, :], scaled_two, 0.0), axis=1),
        ),
        "mp",
    )
    inverse_cube = inverse_two**3 / D
    grad_full = (
        inverse_two[:, None] * scaled_two - full_two * (inverse_cube * projected_two)[:, None]
    )
    grad_pad = inverse_two * pad_term + total_one * inverse_cube * projected_two
    grad_one = gradients + jnp.where(stored[None, :], grad_full - grad_pad[:, None], 0.0)
    stored_total = grad_total + inverse_two * scaled_total - D * grad_pad
    grad_branch_one = grad_one - stored_total[:, None] / D
    output_bias_grad = jnp.sum(grad_branch_one, axis=0)
    rows_grad_one = spread_grads(grad_branch_one.astype(jnp.bfloat16))
    output_weight_grad = jnp.einsum(
        "tc,td->cd", mixed, rows_grad_one, preferred_element_type=jnp.float32
    )
    grad_mixed = jnp.einsum(
        "td,cd->tc", rows_grad_one, output_weight, preferred_element_type=jnp.float32
    ).astype(jnp.bfloat16)
    query_grads, key_grads, value_grads = attend_backward(
        queries,
        key_rows,
        value_rows,
        grad_mixed.reshape(row_count, heads_here, HEAD),
        log_totals,
        segment,
        live_rows,
    )
    grad_inputs = (
        jnp.stack([query_grads, key_grads, value_grads])
        .astype(jnp.bfloat16)
        .reshape(3, row_count, width)
    )
    input_bias_grad = jnp.stack(
        [
            jnp.sum(grad_inputs[0], axis=0, dtype=jnp.float32),
            jnp.sum(grad_inputs[2], axis=0, dtype=jnp.float32),
        ]
    )
    input_weight_grad = jnp.einsum(
        "td,cte->cde", rows_one, grad_inputs, preferred_element_type=jnp.float32
    )
    grad_normed_one = feature_sums(
        jnp.einsum("cte,cde->td", grad_inputs, input_weight, preferred_element_type=jnp.float32)
    )
    gain_one_grad = jnp.sum(grad_normed_one * full_one * inverse_one[:, None], axis=0)
    scaled_one = grad_normed_one * gain_one[None, :]
    projected_one, pad_first = lax.psum(
        (
            jnp.sum(scaled_one * full_one, axis=1),
            jnp.sum(jnp.where(pad_mask[None, :], scaled_one, 0.0), axis=1),
        ),
        "mp",
    )
    inverse_first = inverse_one**3 / D
    grad_first = (
        inverse_one[:, None] * scaled_one - full_one * (inverse_first * projected_one)[:, None]
    )
    grad_pad_first = inverse_one * pad_first + row_total * inverse_first * projected_one
    residual_grad = (
        grad_one + jnp.where(stored[None, :], grad_first - grad_pad_first[:, None], 0.0)
    ).astype(jnp.bfloat16)
    (
        input_weight_grad,
        input_bias_grad,
        output_weight_grad,
        output_bias_grad,
        gain_one_grad,
        gain_two_grad,
        expand_weight_grad,
        expand_bias_grad,
        reduce_weight_grad,
        reduce_bias_grad,
        square_total,
    ) = lax.psum(
        (
            input_weight_grad,
            input_bias_grad,
            output_weight_grad,
            output_bias_grad,
            gain_one_grad,
            gain_two_grad,
            expand_weight_grad,
            expand_bias_grad,
            reduce_weight_grad,
            reduce_bias_grad,
            square_part,
        ),
        "dp",
    )
    residual_rms = jnp.sqrt(square_total / (D * live_count.astype(jnp.float32)))
    return (
        residual_out,
        residual_grad,
        input_weight_grad,
        input_bias_grad,
        output_weight_grad,
        output_bias_grad,
        gain_one_grad,
        gain_two_grad,
        expand_weight_grad,
        expand_bias_grad,
        reduce_weight_grad,
        reduce_bias_grad,
        residual_rms,
        live_count,
    )


def solution(mesh):
    return jax.shard_map(
        on_device,
        mesh=mesh,
        in_specs=(
            P("dp", "mp"),
            P("dp", None),
            P("mp"),
            P(None, None, "mp"),
            P(None, "mp"),
            P("mp", None),
            P("mp"),
            P("mp"),
            P(None, "mp"),
            P("mp"),
            P("mp", None),
            P("mp"),
            P("dp", "mp"),
        ),
        out_specs=(
            P("dp", "mp"),
            P("dp", "mp"),
            P(None, None, "mp"),
            P(None, "mp"),
            P("mp", None),
            P("mp"),
            P("mp"),
            P("mp"),
            P(None, "mp"),
            P("mp"),
            P("mp", None),
            P("mp"),
            P(),
            P(),
        ),
        check_vma=False,
    )
```

profile of v0, /device:TPU:0, one launch (start us, length us, event | category | flops | bytes accessed | tf_op | source)
XLA Modules:
  0.0 926.3 jit_solution(2679985542805380478)
XLA Ops:
  9.9 12.7 %all-reduce.5 = (f32[2048]{0:T(1024)S(1)}, f32[2048]{0:T(1024)S(1)}) all-reduce(f32[2048]{0:T(1024)S(1)} %get-tuple-element.593, f32[2048]{0:T(1024)S(1)} %get-tuple-element.592), channel_id=1, replica_groups=mesh['dp'=8,'mp'=4] {'mp'}, use_global_device_ids=true, to_apply=%region_5.6 | all-reduce | flops 4096 | bytes 32768 | tf_op jit(solution)/shard_map/psum | solution.py:45
  27.5 27.2 %all-gather.5.cloned.1.call-done = bf16[2048,768]{0,1:T(8,128)(2,1)} async-done(((bf16[2048,192]{0,1:T(8,128)(2,1)}), bf16[2048,768]{0,1:T(8,128)(2,1)}) %all-gather.5.cloned.1.call-update) | async-done | bytes 3145744 | tf_op jit(solution)/shard_map/all_gather | solution.py:49
  59.4 94.8 %while.38 = (s32[]{:T(128)}, bf16[4,512,3,64]{1,3,2,0:T(8,128)(2,1)}, f32[4,3,512]{2,1,0:T(4,128)}, s32[4]{0:T(128)S(1)}, s32[2048]{0:T(1024)S(1)}, /*index=5*/p...) while((s32[]{:T(128)}, ...), condition=%wide.region_9.10_spmd, body=%wide.region_6.9_spmd.sunk | while | flops 849445888 | bytes 43996932 | solution.py:104
  75.2 7.3 fusion.151
  98.9 7.3 fusion.151
  122.6 7.3 fusion.151
  146.2 7.3 fusion.151
  161.1 58.5 %reduce-scatter.5.cloned.1.call-done = f32[2048,192]{0,1:T(8,128)} async-done(((f32[2048,768]{0,1:T(8,128)}), f32[2048,192]{0,1:T(8,128)}) %reduce-scatter.5.cloned.1.call-update) | async-done | bytes 1572880 | tf_op jit(solution)/shard_map/reduce_scatter | solution.py:54
  221.7 6.8 psum.184
  233.5 11.0 %all-reduce.4 = (f32[2048]{0:T(1024)}, f32[2048]{0:T(1024)}, f32[2048]{0:T(1024)}) all-reduce(f32[2048]{0:T(1024)} %get-tuple-element.588, f32[2048]{0:T(1024)} %get-tuple-element.587, f32[2048]{0:T(1024)S(1)} %copy-done.36), channel_id=1, replica_groups=mesh['dp'=8,'mp'=4] {'mp'}, use_global_device_ids=true, to_apply=%region_16.17 | all-reduce | flops 6144 | bytes 49152 | tf_op jit(solution)/shard_map/psum | solution.py:45
  251.6 27.4 %all-gather.7.cloned.1.call-done = bf16[2048,768]{0,1:T(8,128)(2,1)} async-done(((bf16[2048,192]{0,1:T(8,128)(2,1)}), bf16[2048,768]{0,1:T(8,128)(2,1)}) %all-gather.7.cloned.1.call-update) | async-done | bytes 3145744 | tf_op jit(solution)/shard_map/all_gather | solution.py:49
  279.0 7.5 fusion.95
  286.5 23.1 %all-gather.9.cloned.1.call-done = bf16[2048,768]{0,1:T(8,128)(2,1)} async-done(((bf16[2048,192]{0,1:T(8,128)(2,1)}), bf16[2048,768]{0,1:T(8,128)(2,1)}) %all-gather.9.cloned.1.call-update) | async-done | bytes 3145744 | tf_op jit(solution)/shard_map/all_gather | solution.py:60
  309.6 12.7 %convert_reduce_fusion = (f32[768]{0:T(1024)}, bf16[2048,768]{1,0:T(8,128)(2,1)S(1)}, bf16[2048,768]{1,0:T(8,128)(2,1)}) fusion(f32[2048,768]{1,0:T(8,128)} %fusion.95, f32[768]{0:T(1024)} %param.26, bf16[2048,768]{0,1:T(8,128)(2,1)} %all-gather.9.cloned.1.call-done, bf16[768,768]{1,0:T(8,128)(2,1)S(1)} %copy-done), kind=kOutput, calls=%fused_computation.58 | convolution fusion | flops 2455239936 | bytes 16914432 | tf_op jit(solution)/shard_map/td,fd->tf/dot_general | solution.py:219
  334.8 31.4 %reduce-scatter.9.cloned.1.call-done = bf16[2048,192]{0,1:T(8,128)(2,1)} async-done(((bf16[2048,768]{0,1:T(8,128)(2,1)}), bf16[2048,192]{0,1:T(8,128)(2,1)}) %reduce-scatter.9.cloned.1.call-update) | async-done | bytes 786448 | tf_op jit(solution)/shard_map/reduce_scatter | solution.py:64
  369.5 57.5 %reduce-scatter.7.cloned.1.call-done = f32[2048,192]{0,1:T(8,128)} async-done(((f32[2048,768]{0,1:T(8,128)}), f32[2048,192]{0,1:T(8,128)}) %reduce-scatter.7.cloned.1.call-update) | async-done | bytes 1572880 | tf_op jit(solution)/shard_map/reduce_scatter | solution.py:54
  428.6 10.3 %all-reduce.3 = (f32[2048]{0:T(1024)S(1)}, f32[2048]{0:T(1024)S(1)}, f32[2048]{0:T(1024)S(1)}, f32[2048]{0:T(1024)S(1)}) all-reduce(f32[2048]{0:T(1024)S(1)} %add_reduce_fusion, f32[2048]{0:T(1024)S(1)} %get-tuple-element.582, f32[2048]{0:T(1024)S(1)} %get-tuple-element.590, ...), channel_id=1, replica_groups=mesh['dp'=8,'mp'=4] {'mp'}, use_global_device_ids=true, to_apply=%region_19.20 | all-reduce | flops 8192 | bytes 65536 | tf_op jit(solution)/shard_map/psum | solution.py:77
  446.1 29.7 %all-gather.11.cloned.1.call-done = bf16[2048,768]{0,1:T(8,128)(2,1)} async-done(((bf16[2048,192]{0,1:T(8,128)(2,1)}), bf16[2048,768]{0,1:T(8,128)(2,1)}) %all-gather.11.cloned.1.call-update) | async-done | bytes 3145744 | tf_op jit(solution)/shard_map/all_gather | solution.py:60
  479.5 144.6 %while.39 = (s32[]{:T(128)}, bf16[2048,3,64]{0,2,1:T(8,128)(2,1)}, f32[2048,3,64]{0,2,1:T(8,128)}, f32[2048,3,64]{0,2,1:T(8,128)}, s32[2048]{0:T(1024)S(1)}, /*i...) while((s32[]{:T(128)}, bf16[2048,3,64]{0,2,1:T(8,128)(2,1)}, ...), condition=%wide.region_31.32_spmd.clone, body=%wide.region_29.31_spmd.clone.sunk | while | flops 2068808704 | bytes 156712976 | solution.py:148
  630.6 7.0 fusion.99
  648.2 12.0 %psum.207 = s32[]{:T(128)} all-reduce(s32[]{:T(128)} %reduce_sum.273), channel_id=1, replica_groups=mesh['dp'=8,'mp'=4] {'dp'}, use_global_device_ids=true, to_apply=%region_61.62 | all-reduce | flops 1 | bytes 8 | tf_op jit(solution)/shard_map/psum | solution.py:170
  671.0 10.3 %all-reduce.2 = (f32[2048]{0:T(1024)S(1)}, f32[2048]{0:T(1024)S(1)}, f32[2048]{0:T(1024)S(1)}, f32[2048]{0:T(1024)S(1)}) all-reduce(f32[2048]{0:T(1024)S(1)} %get-tuple-element.584, f32[2048]{0:T(1024)S(1)} %get-tuple-element.589, f32[2048]{0:T(1024)S(1)} %copy-done.37, f32[2048]{0:T(1024)S(1)} %copy-done.38), channel_id=1, replica_groups=mesh['dp'=8,'mp'=4] {'mp'}, use_global_device_ids=true, to_apply=%region_34.35 | all-reduce | flops 8192 | bytes 65536 | tf_op jit(solution)/shard_map/psum | solution.py:284
  682.5 39.7 %all-reduce = (f32[2,192]{1,0:T(2,128)}, f32[192]{0:T(256)}, f32[192]{0:T(256)}, f32[192]{0:T(256)}, f32[768]{0:T(1024)}, /*index=5*/f32[192]{0:T(256)}, f32[]{:T(128)}) all-reduce(f32[2,192]{1,0:T(2,128)S(1)} %pad_maximum_fusion.3, f32[192]{0:T(256)S(1)} %copy-done.52, ...), channel_id=1, replica_groups=mesh['dp'=8,'mp'=4] {'dp'}, use_global_device_ids=true, to_apply=%region_40.41 | all-reduce | flops 1921 | bytes 15368 | tf_op jit(solution)/shard_map/psum | solution.py:311
  726.0 184.6 %all-reduce.8.cloned.1.call-done = (f32[3,768,192]{1,2,0:T(8,128)}, f32[192,768]{1,0:T(8,128)}, f32[768,768]{1,0:T(8,128)}, f32[768,768]{1,0:T(8,128)}) async-done(((f32[3,768,192]{1,2,0:T(8,128)}, f32[192,768]{1,0:T(8,128)}, f32[768,768]{1,0:T(8,128)}, f32[768,768]{1,0:T(8,128)}), (f32[3,768,192]{1,2,0:T(8,128)}, f32[192,768]{1,0:T(8,128)}, f32[768,768]{1,0:T(8,128)}, ...) | async-done | bytes 7077904 | tf_op jit(solution)/shard_map/psum | solution.py:311
  (345 shorter events, 297.3 us)
Async XLA Ops:
  7.2 302.5 %copy-start = (bf16[768,768]{1,0:T(8,128)(2,1)S(1)}, bf16[768,768]{1,0:T(8,128)(2,1)}, u32[]{:S(2)}) copy-start(bf16[768,768]{1,0:T(8,128)(2,1)} %param.27) | copy-start | bytes 3538948
  7.2 47.5 %copy-start.61 = (bf16[3,768,192]{1,2,0:T(8,128)(2,1)S(1)}, bf16[3,768,192]{1,2,0:T(8,128)(2,1)}, u32[]{:S(2)}) copy-start(bf16[3,768,192]{1,2,0:T(8,128)(2,1)} %param.20) | copy-start | bytes 2654212
  7.2 47.4 %all-gather.5.cloned.1.call-start = ((), (), s32[]{:S(2)}) async-start(), calls=%async_computation.4 | async-start | bytes 3932160 | tf_op jit(solution)/shard_map/all_gather | solution.py:49
  7.3 51.3 %copy-start.43 = (pred[192]{0:T(512)(128)(4,1)}, pred[192]{0:T(512)(128)(4,1)S(1)}, u32[]{:S(2)}) copy-start(pred[192]{0:T(512)(128)(4,1)S(1)} %get-tuple-element.690) | copy-start | bytes 580
  7.3 51.3 %copy-start.46 = (pred[192]{0:T(512)(128)(4,1)}, pred[192]{0:T(512)(128)(4,1)S(1)}, u32[]{:S(2)}) copy-start(pred[192]{0:T(512)(128)(4,1)S(1)} %get-tuple-element.689) | copy-start | bytes 580
  22.6 36.0 %copy-start.41 = (f32[2048]{0:T(1024)}, f32[2048]{0:T(1024)S(1)}, u32[]{:S(2)}) copy-start(f32[2048]{0:T(1024)S(1)} %get-tuple-element.661) | copy-start | bytes 24580
  25.7 193.9 %reduce-scatter.5.cloned.1.call-start = ((), (), s32[]{:S(2)}) async-start(), calls=%async_computation.5 | async-start | bytes 7864320 | tf_op jit(solution)/shard_map/reduce_scatter | solution.py:54
  161.0 58.5 %copy-start.54 = (f32[192]{0:T(256)S(1)}, f32[192]{0:T(256)}, u32[]{:S(2)}) copy-start(f32[192]{0:T(256)} %param.23) | copy-start | bytes 2308
  161.0 68.2 %copy-start.9 = (bf16[2048,192]{0,1:T(8,128)(2,1)S(1)}, bf16[2048,192]{0,1:T(8,128)(2,1)}, u32[]{:S(2)}) copy-start(bf16[2048,192]{0,1:T(8,128)(2,1)} %param.17) | copy-start | bytes 2359300
  161.0 118.0 %all-gather.7.cloned.1.call-start = ((), (), s32[]{:S(2)}) async-start(), calls=%async_computation.6 | async-start | bytes 3932160 | tf_op jit(solution)/shard_map/all_gather | solution.py:49
  248.4 61.2 %all-gather.9.cloned.1.call-start = ((), (), s32[]{:S(2)}) async-start(), calls=%async_computation.8 | async-start | bytes 3932160 | tf_op jit(solution)/shard_map/all_gather | solution.py:60
  251.6 114.6 %reduce-scatter.9.cloned.1.call-start = ((), (), s32[]{:S(2)}) async-start(), calls=%async_computation.9 | async-start | bytes 3932160 | tf_op jit(solution)/shard_map/reduce_scatter | solution.py:64
  328.1 98.9 %reduce-scatter.7.cloned.1.call-start = ((), (), s32[]{:S(2)}) async-start(), calls=%async_computation.7 | async-start | bytes 7864320 | tf_op jit(solution)/shard_map/reduce_scatter | solution.py:54
  334.7 92.3 %copy-start.55 = (f32[192]{0:T(256)S(1)}, f32[192]{0:T(256)}, u32[]{:S(2)}) copy-start(f32[192]{0:T(256)} %param.28) | copy-start | bytes 2308
  334.7 104.2 %copy-start.39 = (f32[2048]{0:T(1024)S(1)}, f32[2048]{0:T(1024)}, u32[]{:S(2)}) copy-start(f32[2048]{0:T(1024)} %get-tuple-element.659) | copy-start | bytes 24580
  334.7 104.2 %copy-start.40 = (f32[2048]{0:T(1024)S(1)}, f32[2048]{0:T(1024)}, u32[]{:S(2)}) copy-start(f32[2048]{0:T(1024)} %get-tuple-element.658) | copy-start | bytes 24580
  334.7 104.2 %copy-start.44 = (pred[192]{0:T(512)(128)(4,1)S(1)}, pred[192]{0:T(512)(128)(4,1)}, u32[]{:S(2)}) copy-start(pred[192]{0:T(512)(128)(4,1)} %copy-done.43) | copy-start | bytes 580
  334.7 141.1 %all-gather.11.cloned.1.call-start = ((), (), s32[]{:S(2)}) async-start(), calls=%async_computation.10 | async-start | bytes 3932160 | tf_op jit(solution)/shard_map/all_gather | solution.py:60
  366.2 72.8 %copy-start.21 = (bf16[2048,192]{0,1:T(8,128)(2,1)S(1)}, bf16[2048,192]{0,1:T(8,128)(2,1)}, u32[]{:S(2)}) copy-start(bf16[2048,192]{0,1:T(8,128)(2,1)} %reduce-scatter.9.cloned.1.call-done) | copy-start | bytes 2359300
  446.1 222.5 %reduce-scatter.11.cloned.1.call-start = ((), (), s32[]{:S(2)}) async-start(), calls=%async_computation.11 | async-start | bytes 3932160 | tf_op jit(solution)/shard_map/reduce_scatter | solution.py:64
  630.5 280.1 %all-reduce.8.cloned.1.call-start = ((), (), s32[]{:S(2)}) async-start(), calls=%async_computation.12 | async-start | bytes 14155776 | tf_op jit(solution)/shard_map/psum | solution.py:311
  647.6 35.0 %copy-start.52 = (f32[192]{0:T(256)S(1)}, f32[192]{0:T(256)}, u32[]{:S(2)}) copy-start(f32[192]{0:T(256)} %get-tuple-element.664) | copy-start | bytes 2308
  647.6 75.4 %copy-start.42 = (f32[2048]{0:T(1024)S(1)}, f32[2048]{0:T(1024)}, u32[]{:S(2)}) copy-start(f32[2048]{0:T(1024)} %copy-done.41) | copy-start | bytes 24580
  647.6 75.4 %copy-start.12 = (f32[2048,192]{0,1:T(8,128)S(1)}, f32[2048,192]{0,1:T(8,128)}, u32[]{:S(2)}) copy-start(f32[2048,192]{0,1:T(8,128)} %copy-done.11) | copy-start | bytes 4718596
  (76 other events, 722.3 us)
Sparse Core Ops, SparseCore 0:
  25.8 28.8 all-gather.4
  161.2 58.3 reduce-scatter.4
  248.5 30.4 all-gather.6
  281.1 28.5 all-gather.8
  328.2 37.9 reduce-scatter.8
  368.6 58.3 reduce-scatter.6
  446.2 29.5 all-gather.10
  630.6 37.9 reduce-scatter.10
  674.2 236.3 all-reduce.7
where the time goes:
time: 936 us; the launch traced here: 926 us
  waiting for transfers between devices  446 us (48%)
  matrix products  212 us (23%)
  other arithmetic  107 us (11%)
  blocking collectives  103 us (11%)
  local copies, waits for them, and re-layouts  28.5 us (3%)
  between operations  17.3 us (2%)
  loops' own time  13 us (1%)
    psum x1, waiting for transfers between devices, on_device(): lax.psum((input_weight_grad, input_bias_grad, output_weight_grad, output_...  185 us
    reduce_scatter x2, waiting for transfers between devices, sum_branch(): lax.psum_scatter(partial_rows, 'mp', scatter_dimension=1, tiled=True)  116 us
    all_gather x2, waiting for transfers between devices, gather_normed(): return lax.all_gather(normed, 'mp', axis=1, tiled=True)  54.6 us
    all_gather x2, waiting for transfers between devices, spread_grads(): return lax.all_gather(grad_rows, 'mp', axis=1, tiled=True)  52.8 us
    psum x1, blocking collectives, on_device(): lax.psum((input_weight_grad, input_bias_grad, output_weight_grad, output_...  39.7 us
    reduce_scatter x2, waiting for transfers between devices, feature_sums(): lax.psum_scatter(partial_rows.astype(jnp.bfloat16), 'mp', scatter_dimensi...  37.6 us
    dot_general x4, matrix products, attend_block(): jnp.einsum('hqk,khd->qhd', attn_probs, value_rows, preferred_element_type...  29.3 us
    reduce_sum x4, other arithmetic, attend_block(): row_sum = jnp.sum(weights, axis=2, keepdims=True)  27.1 us
  transfers between devices with their start and end apart: 9, of which 9 were waited for; matrix products, arithmetic and copies ran while one was open for 5% of the time, Pallas kernels for 0%

commit v1 on v0

v1 whole, which is shorter than its diff:
```python
import functools

import jax
import jax.numpy as jnp
from jax import lax
from jax.experimental import pallas as pl
from jax.experimental.pallas import tpu as pltpu
from jax.sharding import PartitionSpec as P

D = 768
HEAD = 64
SHORT = 512
LONG = 2048
EPSILON = 1e-05
SCORE_SCALE = 0.125
FAR = 1e30

F32 = jnp.float32
BF16 = jnp.bfloat16
VMEM = pltpu.VMEM
SMEM = pltpu.SMEM
NT = (((1,), (1,)), ((), ()))
TN = (((0,), (0,)), ((), ()))


def dot(a, b):
    return jnp.dot(a, b, preferred_element_type=F32)


def dot_nt(a, b):
    return lax.dot_general(a, b, NT, preferred_element_type=F32)


def dot_tn(a, b):
    return lax.dot_general(a, b, TN, preferred_element_type=F32)


def lanes(shape):
    return lax.broadcasted_iota(jnp.int32, shape, 1)


def rows_of(shape):
    return lax.broadcasted_iota(jnp.int32, shape, 0)


def decompress(raw):
    pad = lanes(raw.shape) == D - 1
    kept = jnp.where(pad, 0.0, raw)
    full = jnp.where(pad, -jnp.sum(kept, axis=1, keepdims=True), kept)
    inverse = lax.rsqrt(jnp.mean(full * full, axis=1, keepdims=True) + EPSILON)
    return full, inverse


def center(rows):
    return rows - jnp.mean(rows, axis=1, keepdims=True)


def branch_grad(raw):
    pad = lanes(raw.shape) == D - 1
    return center(jnp.where(pad, 0.0, raw))


def head_of(values, head):
    return jnp.where(lanes(values.shape) // HEAD == head, values, jnp.zeros_like(values))


def flags(lengths_ref):
    total = lengths_ref[0, 0]
    for slot in range(1, lengths_ref.shape[1]):
        total = total + lengths_ref[0, slot]
    return lengths_ref[0, 0] == LONG, total


def diagonal(live, transposed):
    a = rows_of((SHORT, SHORT))
    b = lanes((SHORT, SHORT))
    query, key = (b, a) if transposed else (a, b)
    return (key == query) | ((key < query) & live)


def forward_kernel(
    lengths_ref, res_ref, gain_ref, w_ref, bias_ref,
    q_ref, k_ref, v_ref, mixed_ref, lse_ref, k_s, v_s,
):
    i = pl.program_id(0)
    heads = q_ref.shape[1] // HEAD
    width = q_ref.shape[1]
    full, inverse = decompress(res_ref[...].astype(F32))
    rows = (full * inverse * gain_ref[...]).astype(BF16)
    q = (dot(rows, w_ref[0]) + bias_ref[0:1]).astype(BF16)
    k = dot(rows, w_ref[1]).astype(BF16)
    v = (dot(rows, w_ref[2]) + bias_ref[1:2]).astype(BF16)
    q_ref[...] = q
    k_ref[...] = k
    v_ref[...] = v
    v_ext = jnp.concatenate([v, jnp.ones((SHORT, HEAD), BF16)], axis=1)
    here = pl.ds(pl.multiple_of(i * SHORT, SHORT), SHORT)
    k_s[here] = k
    v_s[here] = v_ext
    is_long, total = flags(lengths_ref)
    live = i * SHORT < total
    far = jnp.where(is_long, 0.0, FAR)
    allowed = diagonal(live, False)
    scaled = q * SCORE_SCALE
    q_heads = [head_of(scaled, h) for h in range(heads)]

    carry = []
    for h in range(heads):
        s = jnp.where(allowed, dot_nt(q_heads[h], k), -FAR)
        m = jnp.max(s, axis=1, keepdims=True)
        p = jnp.exp(s - m).astype(BF16)
        carry.append((m, dot(p, v_ext)))

    def body(j, carry):
        there = pl.ds(pl.multiple_of(j * SHORT, SHORT), SHORT)
        k_j = k_s[there]
        v_j = v_s[there]
        out = []
        for h in range(heads):
            m, acc = carry[h]
            s = dot_nt(q_heads[h], k_j)
            new = jnp.maximum(m, jnp.max(s, axis=1, keepdims=True) - far)
            p = jnp.exp(s - (new + far)).astype(BF16)
            out.append((new, acc * jnp.exp(m - new) + dot(p, v_j)))
        return out

    carry = lax.fori_loop(0, i, body, carry)
    mixed = jnp.zeros((SHORT, width), F32)
    lse = jnp.zeros((SHORT, 128), F32)
    for h in range(heads):
        m, acc = carry[h]
        norm = acc[:, width : width + 1]
        mixed = mixed + head_of(acc[:, :width] / norm, h)
        lse = jnp.where(lanes(lse.shape) == h, m + jnp.log(norm), lse)
    mixed_ref[...] = mixed.astype(BF16)
    lse_ref[...] = jnp.transpose(lse)[:8]


def middle_kernel(
    res_ref, cot_ref, mixed_ref, wo_ref, bo_ref, gain_ref, we_ref, be_ref, wr_ref,
    x1_ref, b2_ref, e2_ref, gwe_ref, gwr_ref, gbe_ref, gbr_ref, gwe_s, gwr_s,
):
    i = pl.program_id(0)

    @pl.when(i == 0)
    def _():
        gwe_s[...] = jnp.zeros_like(gwe_s)
        gwr_s[...] = jnp.zeros_like(gwr_s)
        gbe_ref[...] = jnp.zeros_like(gbe_ref)
        gbr_ref[...] = jnp.zeros_like(gbr_ref)

    full, _ = decompress(res_ref[...].astype(F32))
    x1 = full + center(dot(mixed_ref[...], wo_ref[...]) + bo_ref[...])
    x1_ref[...] = x1
    inverse = lax.rsqrt(jnp.mean(x1 * x1, axis=1, keepdims=True) + EPSILON)
    rows = (x1 * inverse * gain_ref[...]).astype(BF16)
    z = dot(rows, we_ref[...]) + be_ref[...]
    t = jnp.tanh(0.7978845608 * (z + 0.044715 * (z * z * z)))
    active = (0.5 * z * (1.0 + t)).astype(BF16)
    slope = 0.5 * (1.0 + t) + 0.5 * z * (1.0 - t * t) * (
        0.7978845608 * (1.0 + (3 * 0.044715) * (z * z))
    )
    b2_ref[...] = center(dot(active, wr_ref[...])).astype(BF16)
    g2 = branch_grad(cot_ref[...].astype(F32))
    gbr_ref[...] += jnp.sum(g2, axis=0, keepdims=True)
    g2 = g2.astype(BF16)
    gwr_s[...] += dot_tn(active, g2)
    d_hidden = (dot_nt(g2, wr_ref[...]) * slope).astype(BF16)
    gbe_ref[...] += jnp.sum(d_hidden.astype(F32), axis=0, keepdims=True)
    gwe_s[...] += dot_tn(rows, d_hidden)
    e2_ref[...] = dot_nt(d_hidden, we_ref[...]).astype(BF16)

    @pl.when(i == pl.num_programs(0) - 1)
    def _():
        gwe_ref[...] = gwe_s[...].astype(BF16)
        gwr_ref[...] = gwr_s[...].astype(BF16)


def backward_kernel(
    parts, lengths_ref, res_ref, cot_ref, x1_ref, e2_ref, q_ref, mixed_ref, lse_ref, k_ref, v_ref,
    gain_one_ref, gain_ref, w_ref, wo_ref,
    e1_ref, own_ref, tok_ref, gw_ref, gwo_ref, gb_ref, gbo_ref, gg_ref,
    dk_s, dv_s, gw_s, gwo_s,
):
    step = pl.program_id(0)
    i = pl.num_programs(0) - 1 - step
    width = q_ref.shape[1]
    heads = width // HEAD

    @pl.when(step == 0)
    def _():
        for ref in (dk_s, dv_s, gw_s, gwo_s, gb_ref, gbo_ref, gg_ref):
            ref[...] = jnp.zeros_like(ref)

    x1 = x1_ref[...]
    inverse = lax.rsqrt(jnp.mean(x1 * x1, axis=1, keepdims=True) + EPSILON)
    e2 = e2_ref[...].astype(F32)
    gg_ref[...] += jnp.sum(e2 * x1 * inverse, axis=0, keepdims=True)
    c = e2 * gain_ref[...]
    along = jnp.sum(c * x1, axis=1, keepdims=True)
    du = inverse * c - x1 * (inverse * inverse * inverse * along / D)
    g1 = branch_grad(cot_ref[...].astype(F32)) + center(du)
    gbo_ref[...] += jnp.sum(g1, axis=0, keepdims=True)
    g1_last = g1[:, D - 1 :]
    me = lax.axis_index("mp")
    for part in range(parts):

        @pl.when(me == part)
        def _():
            own_ref[...] = g1[:, part * width : (part + 1) * width]

    g1 = g1.astype(BF16)
    mixed = mixed_ref[...]
    gwo_s[...] += dot_tn(mixed, g1)
    d_mixed = dot_nt(g1, wo_ref[...]).astype(BF16)

    product = d_mixed.astype(F32) * mixed.astype(F32)
    product = jnp.transpose(jnp.concatenate([product, jnp.zeros((SHORT, HEAD), F32)], axis=1))
    delta = [
        jnp.sum(product[h * HEAD : (h + 1) * HEAD], axis=0, keepdims=True) for h in range(heads)
    ]
    lse = [lse_ref[h : h + 1] for h in range(heads)]
    is_long, total = flags(lengths_ref)
    live = i * SHORT < total
    far = jnp.where(is_long, 0.0, FAR)
    scaled = q_ref[...] * SCORE_SCALE
    q_heads = [head_of(scaled, h) for h in range(heads)]
    g_heads = [head_of(d_mixed, h) for h in range(heads)]
    q_stack = jnp.concatenate(q_heads, axis=0)
    g_stack = jnp.concatenate(g_heads, axis=0)

    def pair(there, lse, allowed):
        k_j = k_ref[there]
        v_j = v_ref[there]
        probs, scores = [], []
        for h in range(heads):
            p = jnp.exp(dot_nt(k_j, q_heads[h]) - lse[h])
            if allowed is not None:
                p = jnp.where(allowed, p, 0.0)
            probs.append(p.astype(BF16))
            scores.append((p * (dot_nt(v_j, g_heads[h]) - delta[h])).astype(BF16))
        dv_s[there] += dot(jnp.concatenate(probs, axis=1), g_stack)
        dk_s[there] += dot(jnp.concatenate(scores, axis=1), q_stack)
        k_scaled = k_j * SCORE_SCALE
        k_stack = jnp.concatenate([head_of(k_scaled, h) for h in range(heads)], axis=0)
        return dot_tn(jnp.concatenate(scores, axis=0), k_stack)

    here = pl.ds(pl.multiple_of(i * SHORT, SHORT), SHORT)
    dq = pair(here, lse, diagonal(live, True))
    lse_far = [row + far for row in lse]

    def body(j, dq):
        return dq + pair(pl.ds(pl.multiple_of(j * SHORT, SHORT), SHORT), lse_far, None)

    dq = lax.fori_loop(0, i, body, dq).astype(BF16)
    dk = dk_s[here].astype(BF16)
    dv = dv_s[here].astype(BF16)
    gb_ref[0:1] += jnp.sum(dq.astype(F32), axis=0, keepdims=True)
    gb_ref[1:2] += jnp.sum(dv.astype(F32), axis=0, keepdims=True)

    full, inverse = decompress(res_ref[...].astype(F32))
    rows = (full * inverse * gain_one_ref[...]).astype(BF16)
    e1 = jnp.zeros((SHORT, D), F32)
    for n, d in enumerate((dq, dk, dv)):
        gw_s[n] += dot_tn(rows, d)
        e1 = e1 + dot_nt(d, w_ref[n])
    c = e1 * gain_one_ref[...]
    along = jnp.sum(c * full, axis=1, keepdims=True)
    e1_ref[...] = e1.astype(BF16)
    lane = lanes((SHORT, 128))
    tok = jnp.zeros((SHORT, 128), F32)
    for n, column in enumerate((along, c[:, D - 1 :], inverse, full[:, D - 1 :], g1_last)):
        tok = jnp.where(lane == n, column, tok)
    tok_ref[...] = tok

    @pl.when(step == pl.num_programs(0) - 1)
    def _():
        gw_ref[...] = gw_s[...].astype(BF16)
        gwo_ref[...] = gwo_s[...].astype(BF16)


def whole(shape):
    return pl.BlockSpec(shape, lambda i: (0,) * len(shape))


def params(limit=60):
    return pltpu.CompilerParams(vmem_limit_bytes=limit << 20)


def on_device(
    residual,
    lengths,
    gain_one,
    input_weight,
    input_bias,
    output_weight,
    output_bias,
    gain_two,
    expand_weight,
    expand_bias,
    reduce_weight,
    reduce_bias,
    cotangent,
):
    count, width = residual.shape
    parts = D // width
    hidden = expand_weight.shape[1]
    blocks = count // SHORT
    me = lax.axis_index("mp")

    def shape(*dims, dtype=F32):
        return jax.ShapeDtypeStruct(dims, dtype)

    up = lambda w: pl.BlockSpec((SHORT, w), lambda i: (i, 0))
    down = lambda w: pl.BlockSpec((SHORT, w), lambda i: (blocks - 1 - i, 0))
    smem = pl.BlockSpec(memory_space=SMEM)

    def own(vector):
        return lax.dynamic_slice_in_dim(vector, me * width, width, vector.ndim - 1)

    gains = lax.all_gather(
        jnp.stack([gain_one, output_bias, gain_two, reduce_bias]), "mp", axis=1, tiled=True
    )
    res_full = lax.all_gather(residual, "mp", axis=1, tiled=True)
    cot_full = lax.all_gather(cotangent, "mp", axis=1, tiled=True)
    wo_full = lax.all_gather(output_weight, "mp", axis=0, tiled=True)

    q, k, v, mixed, lse = pl.pallas_call(
        forward_kernel,
        grid=(blocks,),
        in_specs=[smem, up(D), whole((1, D)), whole((3, D, width)), whole((2, width))],
        out_specs=[up(width)] * 4 + [pl.BlockSpec((8, SHORT), lambda i: (0, i))],
        out_shape=[shape(count, width, dtype=BF16)] * 4 + [shape(8, count)],
        scratch_shapes=[VMEM((count, width), BF16), VMEM((count, width + HEAD), BF16)],
        compiler_params=params(),
        name="forward",
    )(lengths, res_full, gains[0:1], input_weight, input_bias)

    mixed_full = lax.all_gather(mixed, "mp", axis=1, tiled=True)

    x1, b2, e2, gwe, gwr, gbe, gbr = pl.pallas_call(
        middle_kernel,
        grid=(blocks,),
        in_specs=[up(D)] * 3
        + [whole((D, D)), whole((1, D)), whole((1, D))]
        + [whole((D, hidden)), whole((1, hidden)), whole((hidden, D))],
        out_specs=[up(D)] * 3
        + [whole((D, hidden)), whole((hidden, D)), whole((1, hidden)), whole((1, D))],
        out_shape=[
            shape(count, D),
            shape(count, D, dtype=BF16),
            shape(count, D, dtype=BF16),
            shape(D, hidden, dtype=BF16),
            shape(hidden, D, dtype=BF16),
            shape(1, hidden),
            shape(1, D),
        ],
        scratch_shapes=[VMEM((D, hidden), F32), VMEM((hidden, D), F32)],
        compiler_params=params(),
        name="middle",
    )(
        res_full, cot_full, mixed_full, wo_full, gains[1:2], gains[2:3],
        expand_weight, expand_bias[None], reduce_weight,
    )

    e2 = lax.psum(e2, "mp")
    gwe, gwr = lax.psum((gwe, gwr), "dp")
    b2 = lax.psum_scatter(b2, "mp", scatter_dimension=1, tiled=True)

    e1, g_own, tok, gw, gwo, gb, gbo, gg = pl.pallas_call(
        functools.partial(backward_kernel, parts),
        grid=(blocks,),
        in_specs=[smem, down(D), down(D), down(D), down(D), down(width), down(width)]
        + [pl.BlockSpec((8, SHORT), lambda i: (0, blocks - 1 - i))]
        + [whole((count, width))] * 2
        + [whole((1, D)), whole((1, D)), whole((3, D, width)), whole((width, D))],
        out_specs=[down(D), down(width), down(128)]
        + [whole((3, D, width)), whole((width, D)), whole((2, width)), whole((1, D)), whole((1, D))],
        out_shape=[
            shape(count, D, dtype=BF16),
            shape(count, width),
            shape(count, 128),
            shape(3, D, width, dtype=BF16),
            shape(width, D, dtype=BF16),
            shape(2, width),
            shape(1, D),
            shape(1, D),
        ],
        scratch_shapes=[
            VMEM((count, width), F32),
            VMEM((count, width), F32),
            VMEM((3, D, width), F32),
            VMEM((width, D), F32),
        ],
        compiler_params=params(),
        name="backward",
    )(
        lengths, res_full, cot_full, x1, e2, q, mixed, lse, k, v,
        gains[0:1], gains[2:3], input_weight, output_weight,
    )

    columns = me * width + jnp.arange(width)
    stored = (columns < D - 1)[None, :]
    e1 = lax.psum_scatter(e1, "mp", scatter_dimension=1, tiled=True).astype(F32)
    along, c_last = lax.psum((tok[:, 0], tok[:, 1]), "mp")
    inverse, u_last, g_last = tok[:, 2], tok[:, 3], tok[:, 4]
    u_own = jnp.where(stored, residual.astype(F32), u_last[:, None])
    cube = inverse * inverse * inverse * along / D
    result = g_own + inverse[:, None] * (e1 * gain_one[None]) - u_own * cube[:, None]
    last = g_last + inverse * c_last - u_last * cube
    residual_grad = jnp.where(stored, result - last[:, None], 0.0).astype(BF16)
    gain_one_grad = jnp.sum(e1 * u_own * inverse[:, None], axis=0)

    x2 = own(x1) + b2.astype(F32) + (reduce_bias - jnp.mean(gains[3]))[None]
    residual_out = jnp.where(stored, x2, 0.0).astype(BF16)
    live = jnp.arange(count) < jnp.sum(lengths)
    square = jnp.sum(jnp.where(live[:, None], x2 * x2, 0.0))
    square = lax.psum(square, ("dp", "mp"))
    live_count = lax.psum(jnp.sum(lengths), "dp")
    small = jnp.concatenate(
        [gb.reshape(-1), own(gbo[0]), gain_one_grad, own(gg[0]), gbe[0], own(gbr[0])]
    )
    after = gwe[0, 0] * 0
    gw, gwo = gw + after, gwo + after
    gw, gwo = lax.psum((gw, gwo), "dp")
    small = lax.psum(small, "dp")
    cuts = []
    start = 0
    for size in (2 * width, width, width, width, hidden, width):
        cuts.append(small[start : start + size])
        start += size
    residual_rms = jnp.sqrt(square / (D * live_count.astype(F32)))
    return (
        residual_out,
        residual_grad,
        gw.astype(F32),
        cuts[0].reshape(2, width),
        gwo.astype(F32),
        cuts[1],
        cuts[2],
        cuts[3],
        gwe.astype(F32),
        cuts[4],
        gwr.astype(F32),
        cuts[5],
        residual_rms,
        live_count,
    )


def solution(mesh):
    return jax.shard_map(
        on_device,
        mesh=mesh,
        in_specs=(
            P("dp", "mp"),
            P("dp", None),
            P("mp"),
            P(None, None, "mp"),
            P(None, "mp"),
            P("mp", None),
            P("mp"),
            P("mp"),
            P(None, "mp"),
            P("mp"),
            P("mp", None),
            P("mp"),
            P("dp", "mp"),
        ),
        out_specs=(
            P("dp", "mp"),
            P("dp", "mp"),
            P(None, None, "mp"),
            P(None, "mp"),
            P("mp", None),
            P("mp"),
            P("mp"),
            P("mp"),
            P(None, "mp"),
            P("mp"),
            P("mp", None),
            P("mp"),
            P(),
            P(),
        ),
        check_vma=False,
    )
```

time: 936 us -> 631 us (0.67)
  matrix products: 212 us -> 0 us
  Pallas kernels: 0 us -> 103 us
  other arithmetic: 107 us -> 15.9 us
  waiting for transfers between devices: 446 us -> 357 us
  local copies, waits for them, and re-layouts: 28.5 us -> 45.4 us
  blocking collectives: 103 us -> 88.7 us
  loops' own time: 13 us -> 0 us
    dot_general x39 -> x0, matrix products: 208 us -> none  [the longest x4 29.3 us: attend_block(): jnp.einsum('hqk,khd->qhd', attn_probs, value_rows, preferred_element_type...]
    reduce_scatter x4 -> x0, waiting for transfers between devices: 154 us -> none  [the longest x2 116 us: sum_branch(): lax.psum_scatter(partial_rows, 'mp', scatter_dimension=1, tiled=True)]
    pallas_call x0 -> x3, Pallas kernels: none -> 103 us  [the longest x1 48.3 us: on_device(): pl.pallas_call(functools.partial(backward_kernel, parts), grid=(blocks,),...]
    unnamed x9 -> x11, waiting for transfers between devices: 0.15 us -> 75.4 us
    all_gather x4, waiting for transfers between devices: 107 us -> 59.3 us  [the longest x1 22.6 us: on_device(): mixed_full = lax.all_gather(mixed, 'mp', axis=1, tiled=True)]
    reduce_sum x16 -> x3, other arithmetic: 53.1 us -> 7.31 us  [the longest x1 5.48 us: on_device(): square = jnp.sum(jnp.where(live[:, None], x2 * x2, 0.0))]
    psum x1 -> x3, waiting for transfers between devices: 185 us -> 223 us  [the longest x1 79.3 us: on_device(): gwe, gwr = lax.psum((gwe, gwr), 'dp')]
    convert_element_type x11 -> x3, other arithmetic: 35.5 us -> 4.01 us  [the longest x1 1.58 us: on_device(): gwe.astype(F32)]
  transfers between devices with their start and end apart: 9 -> 9, of which waited for: 9 -> 8; matrix products, arithmetic and copies ran while one was open for 5% -> 7% of each run, Pallas kernels for 0% -> 4%
where the time goes in v1:
time: 631 us; the launch traced here: 629 us
  waiting for transfers between devices  357 us (57%)
  Pallas kernels  103 us (16%)
  blocking collectives  88.7 us (14%)
  local copies, waits for them, and re-layouts  45.4 us (7%)
  between operations  17.9 us (3%)
  other arithmetic  15.9 us (3%)
    psum x1, waiting for transfers between devices, on_device(): gwe, gwr = lax.psum((gwe, gwr), 'dp')  79.3 us
    unnamed x11, waiting for transfers between devices  75.4 us
    psum x1, waiting for transfers between devices, on_device(): gw, gwo = lax.psum((gw, gwo), 'dp')  74.9 us
    psum x1, waiting for transfers between devices, on_device(): e2 = lax.psum(e2, 'mp')  68.3 us
    pallas_call x1, Pallas kernels, on_device(): pl.pallas_call(functools.partial(backward_kernel, parts), grid=(blocks,),...  48.3 us
    psum x1, blocking collectives, on_device(): square = lax.psum(square, ('dp', 'mp'))  37.1 us
    pallas_call x1, Pallas kernels, on_device(): pl.pallas_call(middle_kernel, grid=(blocks,), in_specs=[up(D)] * 3 + [who...  28.9 us
    pallas_call x1, Pallas kernels, on_device(): pl.pallas_call(forward_kernel, grid=(blocks,), in_specs=[smem, up(D), who...  26 us
  transfers between devices with their start and end apart: 9, of which 8 were waited for; matrix products, arithmetic and copies ran while one was open for 7% of the time, Pallas kernels for 4%

profile of v1, /device:TPU:0, one launch (start us, length us, event | category | flops | bytes accessed | tf_op | source)
XLA Modules:
  0.0 629.2 jit_solution(15630473889271937430)
XLA Ops:
  9.5 6.2 all-gather
  18.4 22.5 %all-gather.6.cloned.1.call-done = bf16[2048,768]{0,1:T(8,128)(2,1)} async-done(((bf16[2048,192]{0,1:T(8,128)(2,1)}), bf16[2048,768]{0,1:T(8,128)(2,1)}) %all-gather.6.cloned.1.call-update) | async-done | bytes 3145744 | tf_op jit(solution)/shard_map/all_gather | solution.py:324
  40.8 4.7 copy.47.res_ref
  45.6 26.0 %forward.1 = (bf16[2048,192]{1,0:T(8,128)(2,1)}, bf16[2048,192]{1,0:T(8,128)(2,1)}, bf16[2048,192]{1,0:T(8,128)(2,1)}, bf16[2048,192]{1,0:T(8,128)(2,1)}, f32[8,2048]{1,0:T(8,128)}) custom-call(s32[1,4]{1,0:T(1,128)} %lengths_ref.3, bf16[2048,768]{1,0:T(8,128)(2,1)} %copy.47.res_ref, f32[1,768]{1,0:T(1,128)} %get-tuple-element.115.gain_ref.gain_one_ref, ...), custom_call_target="tpu_custom_call" | custom-call | tf_op jit(solution)/shard_map/forward/pallas_call | solution.py:328
  75.2 4.6 copy.48.cot_ref
  79.9 22.6 %all-gather.10.cloned.1.call-done = bf16[2048,768]{0,1:T(8,128)(2,1)} async-done(((bf16[2048,192]{0,1:T(8,128)(2,1)}), bf16[2048,768]{0,1:T(8,128)(2,1)}) %all-gather.10.cloned.1.call-update) | async-done | bytes 3145744 | tf_op jit(solution)/shard_map/all_gather | solution.py:339
  102.5 4.7 copy.49.mixed_ref
  107.2 14.2 %all-gather.12.cloned.1.call-done.wo_ref = bf16[768,768]{1,0:T(8,128)(2,1)} async-done(((bf16[192,768]{1,0:T(8,128)(2,1)}), bf16[768,768]{1,0:T(8,128)(2,1)}) %all-gather.12.cloned.1.call-update) | async-done | bytes 1179664 | tf_op jit(solution)/shard_map/all_gather | solution.py:326
  121.4 28.9 %middle.1 = (f32[2048,768]{1,0:T(8,128)}, bf16[2048,768]{1,0:T(8,128)(2,1)}, bf16[2048,768]{1,0:T(8,128)(2,1)}, bf16[768,768]{1,0:T(8,128)(2,1)}, bf16[768,768]{...) custom-call(bf16[2048,768]{1,0:T(8,128)(2,1)} %copy.47.res_ref, bf16[2048,768]{1,0:T(8,128)(2,1)} %copy.48.cot_ref, ...), custom_call_target="tpu_custom_call" | custom-call | tf_op jit(solution)/shard_map/middle/pallas_call | solution.py:341
  151.2 79.3 %all-reduce.8.cloned.1.call-done = bf16[768,768]{1,0:T(8,128)(2,1)} async-done(((bf16[768,768]{1,0:T(8,128)(2,1)}), bf16[768,768]{1,0:T(8,128)(2,1)}) %all-reduce.8.cloned.1.call-update) | async-done | bytes 1179664 | tf_op jit(solution)/shard_map/psum | solution.py:367
  232.3 68.3 %all-reduce.6.cloned.1.call-done.e2_ref = bf16[2048,768]{1,0:T(8,128)(2,1)} async-done(((bf16[2048,768]{1,0:T(8,128)(2,1)}), bf16[2048,768]{1,0:T(8,128)(2,1)}) %all-reduce.6.cloned.1.call-update) | async-done | bytes 3145744 | tf_op jit(solution)/shard_map/psum | solution.py:366
  300.7 48.3 %backward.1 = (bf16[2048,768]{1,0:T(8,128)(2,1)}, f32[2048,192]{1,0:T(8,128)}, f32[2048,128]{1,0:T(8,128)}, bf16[3,768,192]{2,1,0:T(8,128)(2,1)}, bf16[192,768]{...) custom-call(s32[1,4]{1,0:T(1,128)} %lengths_ref.3, bf16[2048,768]{1,0:T(8,128)(2,1)} %copy.47.res_ref, ...), custom_call_target="tpu_custom_call" | custom-call | tf_op jit(solution)/shard_map/backward/pallas_call | solution.py:370
  353.4 3.0 copy.57
  358.4 2.9 copy.59
  362.6 13.3 %psum.79 = s32[]{:T(128)} all-reduce(s32[]{:T(128)} %reduce_sum.42), channel_id=1, replica_groups=mesh['dp'=8,'mp'=4] {'dp'}, use_global_device_ids=true, to_apply=%region_15.16 | all-reduce | flops 1 | bytes 8 | tf_op jit(solution)/shard_map/psum | solution.py:419
  381.0 2.5 slice_reduce_fusion.2
  383.5 10.5 %all-reduce = (f32[2048]{0:T(1024)S(1)}, f32[2048]{0:T(1024)S(1)}) all-reduce(f32[2048]{0:T(1024)S(1)} %get-tuple-element.97, f32[2048]{0:T(1024)S(1)} %get-tuple-element.96), channel_id=1, replica_groups=mesh['dp'=8,'mp'=4] {'mp'}, use_global_device_ids=true, to_apply=%region_5.0 | all-reduce | flops 4096 | bytes 32768 | tf_op jit(solution)/shard_map/psum | solution.py:405
  394.8 74.9 %all-reduce.10.cloned.1.call-done = (bf16[3,768,192]{2,1,0:T(8,128)(2,1)}, bf16[192,768]{1,0:T(8,128)(2,1)}, bf16[768,768]{1,0:T(8,128)(2,1)}) async-done(((bf16[3,768,192]{2,1,0:T(8,128)(2,1)}, bf16[192,768]{1,0:T(8,128)(2,1)}, bf16[768,768]{1,0:T(8,128)(2,1)}), (bf16[3,768,192]{2,1,0:T(8,128)(2,1)}, bf16[192,768]{1,0:T(8,128)(2,1)}, bf16[768,768]{1,0:T(8,128)(2,1)})) %all-reduce.10.cloned.1.call-update) | async-done | bytes 2359312 | tf_op jit(solution)/shard_map/psum | solution.py:425
  469.7 2.6 copy.56
  474.8 34.6 %reduce-scatter.7.cloned.1.call-done = bf16[192,2048]{1,0:T(8,128)(2,1)} async-done(((bf16[768,2048]{1,0:T(8,128)(2,1)}), bf16[192,2048]{1,0:T(8,128)(2,1)}) %reduce-scatter.7.cloned.1.call-update) | async-done | bytes 786448
  511.7 38.3 %reduce-scatter.9.cloned.1.call-done = bf16[192,2048]{1,0:T(8,128)(2,1)} async-done(((bf16[768,2048]{1,0:T(8,128)(2,1)}), bf16[192,2048]{1,0:T(8,128)(2,1)}) %reduce-scatter.9.cloned.1.call-update) | async-done | bytes 786448
  552.2 5.5 select_reduce_fusion
  557.7 21.6 %psum.75 = f32[1920]{0:T(1024)S(1)} all-reduce(f32[1920]{0:T(1024)S(1)} %concatenate.3), channel_id=1, replica_groups=mesh['dp'=8,'mp'=4] {'dp'}, use_global_device_ids=true, to_apply=%region_9.10 | all-reduce | flops 1920 | bytes 15360 | tf_op jit(solution)/shard_map/psum | solution.py:426
  583.8 37.1 %psum.78 = f32[]{:T(128)} all-reduce(f32[]{:T(128)} %get-tuple-element.106), channel_id=1, replica_groups=mesh['dp'=8,'mp'=4] {'dp','mp'}, use_global_device_ids=true, to_apply=%region_14.15 | all-reduce | flops 1 | bytes 8 | tf_op jit(solution)/shard_map/psum | solution.py:418
  (81 shorter events, 34.0 us)
Async XLA Ops:
  7.2 8.6 %copy-start.6 = (bf16[3,768,192]{1,2,0:T(8,128)(2,1)S(1)}, bf16[3,768,192]{1,2,0:T(8,128)(2,1)}, u32[]{:S(2)}) copy-start(bf16[3,768,192]{1,2,0:T(8,128)(2,1)} %param.16) | copy-start | bytes 2654212
  7.2 33.7 %all-gather.6.cloned.1.call-start = ((), (), s32[]{:S(2)}) async-start(), calls=%async_computation.2 | async-start | bytes 3932160 | tf_op jit(solution)/shard_map/all_gather | solution.py:324
  7.9 67.3 %all-gather.8.cloned.1.call-start = ((), (), s32[]{:S(2)}) async-start(), calls=%async_computation.3 | async-start | bytes 3932160 | tf_op jit(solution)/shard_map/all_gather | solution.py:325
  8.7 93.8 %all-gather.10.cloned.1.call-start = ((), (), s32[]{:S(2)}) async-start(), calls=%async_computation.4 | async-start | bytes 3932160 | tf_op jit(solution)/shard_map/all_gather | solution.py:339
  71.6 3.0 copy-start.10
  73.8 47.6 %all-gather.12.cloned.1.call-start = ((), (), s32[]{:S(2)}) async-start(), calls=%async_computation.5 | async-start | bytes 1474560 | tf_op jit(solution)/shard_map/all_gather | solution.py:326
  74.4 156.1 %all-reduce.8.cloned.1.call-start = ((), (), s32[]{:S(2)}) async-start(), calls=%async_computation.7 | async-start | bytes 2359296 | tf_op jit(solution)/shard_map/psum | solution.py:367
  150.3 150.3 %all-reduce.6.cloned.1.call-start = ((), (), s32[]{:S(2)}) async-start(), calls=%async_computation.6 | async-start | bytes 6291456 | tf_op jit(solution)/shard_map/psum | solution.py:366
  150.9 318.9 %all-reduce.10.cloned.1.call-start = ((), (), s32[]{:S(2)}) async-start(), calls=%async_computation.10 | async-start | bytes 5308416 | tf_op jit(solution)/shard_map/psum | solution.py:425
  349.0 2.4 copy-start.8
  351.4 2.0 copy-start.2
  352.2 157.3 %reduce-scatter.7.cloned.1.call-start = ((), (), s32[]{:S(2)}) async-start(), calls=%async_computation.8 | async-start | bytes 3932160
  356.4 2.0 copy-start.3
  356.4 193.6 %reduce-scatter.9.cloned.1.call-start = ((), (), s32[]{:S(2)}) async-start(), calls=%async_computation.9 | async-start | bytes 3932160
  361.3 0.7 copy-start.13
  361.3 14.6 %copy-start.1 = (bf16[2048,192]{0,1:T(8,128)(2,1)S(1)}, bf16[2048,192]{0,1:T(8,128)(2,1)}, u32[]{:S(2)}) copy-start(bf16[2048,192]{0,1:T(8,128)(2,1)} %param.13) | copy-start | bytes 2359300
  361.3 17.2 %copy-start.11 = (f32[192]{0:T(256)S(1)}, f32[192]{0:T(256)}, u32[]{:S(2)}) copy-start(f32[192]{0:T(256)} %param.24) | copy-start | bytes 2308
  361.3 17.3 %copy-start.12 = (f32[1,768]{1,0:T(1,128)S(1)}, f32[1,768]{1,0:T(1,128)}, u32[]{:S(2)}) copy-start(f32[1,768]{1,0:T(1,128)} %get-tuple-element.50) | copy-start | bytes 9220
  361.3 18.0 %copy-start.4 = (bf16[768,768]{1,0:T(8,128)(2,1)S(1)}, bf16[768,768]{1,0:T(8,128)(2,1)}, u32[]{:S(2)}) copy-start(bf16[768,768]{1,0:T(8,128)(2,1)} %all-reduce.8.cloned.1.call-done) | copy-start | bytes 3538948
  376.4 4.5 copy-start.14
  376.5 4.6 copy-start
  469.7 2.6 copy-start.7
  469.7 3.5 copy-start.5
  474.8 77.4 %copy-start.9 = (f32[192]{0:T(256)S(1)}, f32[192]{0:T(256)}, u32[]{:S(2)}) copy-start(f32[192]{0:T(256)} %param.15) | copy-start | bytes 2308
Sparse Core Ops, SparseCore 0:
  9.6 31.2 all-gather.5
  42.4 28.5 all-gather.7
  73.9 28.5 all-gather.9
  103.9 17.4 all-gather.11
  150.4 80.0 all-reduce.7
  232.8 67.7 all-reduce.5
  352.3 117.4 all-reduce.9
  472.4 36.9 reduce-scatter.6
  512.0 37.9 reduce-scatter.8

commit v2 on v1

v2 whole, which is shorter than its diff:
```python
import types

import jax
import jax.numpy as jnp
from jax import lax
from jax.experimental import pallas as pl
from jax.experimental.pallas import tpu as pltpu
from jax.sharding import PartitionSpec as P

D = 768
HEAD = 64
SHORT = 512
HALF = SHORT // 2
LONG = 2048
EPSILON = 1e-05
SCORE_SCALE = 0.125
FAR = 1e30
LANES = 128
MESH = pl.DeviceIdType.MESH

F32 = jnp.float32
BF16 = jnp.bfloat16
NT = (((1,), (1,)), ((), ()))
TN = (((0,), (0,)), ((), ()))


def dot(a, b):
    return jnp.dot(a, b, preferred_element_type=F32)


def dot_nt(a, b):
    return lax.dot_general(a, b, NT, preferred_element_type=F32)


def dot_tn(a, b):
    return lax.dot_general(a, b, TN, preferred_element_type=F32)


def lanes(shape):
    return lax.broadcasted_iota(jnp.int32, shape, 1)


def rows_of(shape):
    return lax.broadcasted_iota(jnp.int32, shape, 0)


def at(index, size):
    return pl.ds(pl.multiple_of(index * size, size), size)


def decompress(raw):
    pad = lanes(raw.shape) == D - 1
    kept = jnp.where(pad, 0.0, raw)
    full = jnp.where(pad, -jnp.sum(kept, axis=1, keepdims=True), kept)
    return full, inverse_rms(full)


def inverse_rms(full):
    return lax.rsqrt(jnp.mean(full * full, axis=1, keepdims=True) + EPSILON)


def center(rows):
    return rows - jnp.mean(rows, axis=1, keepdims=True)


def branch_grad(raw):
    pad = lanes(raw.shape) == D - 1
    return center(jnp.where(pad, 0.0, raw))


def head_of(values, head):
    return jnp.where(lanes(values.shape) // HEAD == head, values, jnp.zeros_like(values))


def diagonal(live, transposed):
    a = rows_of((SHORT, SHORT))
    b = lanes((SHORT, SHORT))
    query, key = (b, a) if transposed else (a, b)
    return (key == query) | ((key < query) & live)


def pack(rows):
    tail = rows[:, LANES:]
    return jnp.concatenate(
        [rows[:, :LANES], jnp.concatenate([tail[:HALF], tail[HALF:]], axis=1)], axis=0
    )


def unpack(piece):
    tail = piece[SHORT:]
    tail = jnp.concatenate([tail[:, : LANES // 2], tail[:, LANES // 2 :]], axis=0)
    return jnp.concatenate([piece[:SHORT], tail], axis=1)


PACKED = SHORT + HALF


def copy_to(src, dst, send_sem, recv_sem, peer):
    return pltpu.make_async_remote_copy(
        src_ref=src,
        dst_ref=dst,
        send_sem=send_sem,
        recv_sem=recv_sem,
        device_id={"mp": peer},
        device_id_type=MESH,
    )


class Gather:
    def __init__(self, piece, sems, me, core, across):
        self.piece, self.me, self.core, self.across = piece, me, core, across
        self.send, self.recv = sems

    def copy(self, kind, i):
        slot = self.across if kind == 2 else self.me
        peer = self.across if kind == 1 else self.core
        here = self.piece(slot, i)
        return copy_to(here, here, self.send.at[kind, i], self.recv.at[kind, i], peer)

    def start(self, i):
        self.copy(1, i).start()
        self.copy(0, i).start()

    def forward(self, i):
        self.copy(1, i).wait_recv()
        self.copy(2, i).start()

    def finish(self, i):
        self.copy(0, i).wait_recv()
        self.copy(2, i).wait_recv()

    def drain(self, i):
        for kind in range(3):
            self.copy(kind, i).wait_send()


INPUTS = ("lengths", "res", "cot", "vec", "w", "bias", "wo", "we", "be", "wr")
OUTPUTS = ("out", "grad", "gw", "gwo", "gwe", "gwr", "small")
IN_HBM = ("res", "cot", "wo", "we", "wr", "out", "grad", "gw", "gwo", "gwe", "gwr")


class Reduce:
    def __init__(self, buf, first, second, other, sems, dp, size):
        self.buf, self.first, self.second, self.other = buf, first, second, other
        self.sems = sems
        self.high = buf.shape[0] // 2
        self.count = size // 2
        self.piece = self.high // self.count
        self.side = lax.rem(dp, 2)
        self.place = lax.div(dp, 2)
        self.mate = dp + 1 - 2 * self.side

    def rows(self, p, base=0):
        return pl.ds(pl.multiple_of(base + p * self.piece, self.piece), self.piece)

    def own(self, p):
        return self.buf.at[self.rows(p, self.side * self.high)]

    def copy(self, src, dst, stage, p, slot, peer):
        return pltpu.make_async_remote_copy(
            src_ref=src,
            dst_ref=dst,
            send_sem=self.sems[0].at[stage, p],
            recv_sem=self.sems[1].at[stage, slot],
            device_id={"dp": peer},
            device_id_type=MESH,
        )

    def to_mate(self, p):
        away = self.buf.at[self.rows(p, (1 - self.side) * self.high)]
        return self.copy(away, self.first.at[self.rows(p)], 0, p, p, self.mate)

    def to_owner(self, p, slot):
        return self.copy(
            self.first.at[self.rows(p)], self.second.at[self.rows(slot)], 1, p, slot, 2 * p + self.side
        )

    def to_peer(self, p, slot):
        return self.copy(self.own(slot), self.own(slot), 2, p, slot, 2 * p + self.side)

    def back(self, p):
        return self.copy(self.own(p), self.other.at[self.rows(p)], 3, p, p, self.mate)

    def each(self, body, start=0, stop=None):
        def run(p, _):
            body(p)
            return 0

        lax.fori_loop(start, self.count if stop is None else stop, run, 0)

    def others(self, body):
        def run(p):
            @pl.when(p != self.place)
            def _():
                body(p)

        self.each(run)

    def start(self):
        self.each(lambda p: self.to_mate(p).start())

    def sum_mates(self, p):
        self.to_mate(p).wait_recv()
        here = self.rows(p)
        both = self.buf[self.rows(p, self.side * self.high)].astype(F32) + self.first[here].astype(F32)
        self.first[here] = both.astype(BF16)

        @pl.when(p != self.place)
        def _():
            self.to_owner(p, self.place).start()

    def sum_quarter(self, q):
        self.each(self.sum_mates, q * self.count // 4, (q + 1) * self.count // 4)

    def sum_owners(self):
        self.second[self.rows(self.place)] = self.first[self.rows(self.place)]
        self.others(lambda q: self.to_owner(q, q).wait_recv())
        total = lax.fori_loop(
            0,
            self.count,
            lambda q, acc: acc + self.second[self.rows(q)].astype(F32),
            jnp.zeros((self.piece, self.buf.shape[1]), F32),
        )
        self.buf[self.rows(self.place, self.side * self.high)] = total.astype(BF16)
        self.others(lambda p: self.to_peer(p, self.place).start())
        self.back(self.place).start()

    def forward(self):
        def body(q):
            self.to_peer(q, q).wait_recv()
            self.back(q).start()

        self.others(body)

    def finish(self):
        self.each(lambda p: self.back(p).wait_recv())

    def take(self, body):
        for side in range(2):

            @pl.when(self.side == side)
            def _(side=side):
                body(side, self.buf.at[side * self.high : (side + 1) * self.high])
                body(1 - side, self.other)

    def drain(self):
        self.each(lambda p: self.to_mate(p).wait_send())
        self.others(lambda p: self.to_owner(p, self.place).wait_send())
        self.others(lambda p: self.to_peer(p, self.place).wait_send())
        self.each(lambda p: self.back(p).wait_send())


def scratch(count, width, hidden, groups):
    parts = D // width
    blocks = count // SHORT
    bf, f = BF16, F32
    arrays = dict(
        RES=((parts, blocks * PACKED, LANES), bf),
        COT=((parts, blocks * PACKED, LANES), bf),
        MIX=((parts, blocks * PACKED, LANES), bf),
        VEC=((parts, 8, 2 * LANES), f),
        GAINS=((8, D), f),
        WO=((D, D), bf),
        Q=((count, width), bf),
        K=((count, width), bf),
        VX=((count, width + HEAD), bf),
        LSE=((blocks, 8, SHORT), f),
        X1=((count, D), f),
        E2P=((count, D), bf),
        E2C=((blocks, HALF, D), bf),
        E2Y=((blocks, HALF, D), bf),
        E2T=((blocks, HALF, D), bf),
        PIECES=((2, parts, PACKED, LANES), bf),
        B2C=((2, blocks, PACKED, LANES), bf),
        B2Y=((blocks, PACKED, LANES), bf),
        E1C=((2, blocks, PACKED, LANES), bf),
        E1Y=((blocks, PACKED, LANES), bf),
        STAT=((parts, blocks, 8, SHORT), f),
        DV=((3 * D, width), f),
        GWE=((3 * D, 2 * LANES), f),
        GWR=((3 * D, 2 * LANES), f),
        ACC=((8, D), f),
        BM=((2 * D, hidden), bf),
        BM1=((D, hidden), bf),
        BM2=((D, hidden), bf),
        BM3=((D, hidden), bf),
        BT=((2 * D, 2 * width), bf),
        WE=((D, hidden), bf),
        WR=((hidden, D), bf),
        SMALL=((groups, 16, 2 * LANES), f),
        GB=((8, width), f),
    )
    sems = dict(
        load=(1, 5), store=(1, 8), bm=(4, groups // 2), bt=(4, groups // 2), tiny=(1, groups),
        res=(3, blocks), cot=(3, blocks), mix=(3, blocks), wo_=(3, 1), vec_=(3, 1),
        e2a=(1, blocks), e2x=(1, blocks), e2b=(1, blocks),
        b2c=(2, blocks), b2x=(1, blocks), e1c=(2, blocks), e1x=(1, blocks), stat=(3, blocks),
    )
    names, shapes = [], []
    for name, (shape, dtype) in arrays.items():
        names.append(name)
        shapes.append(pltpu.VMEM(shape, dtype))
    for name, shape in sems.items():
        for way in ("s", "r"):
            names.append(f"{name}_{way}")
            shapes.append(pltpu.SemaphoreType.DMA(shape))
    return names, shapes


def layer_kernel(groups, names, *refs):
    n = types.SimpleNamespace(**dict(zip((*INPUTS, *OUTPUTS, *names), refs, strict=True)))
    count, width = n.res.shape
    parts = D // width
    blocks = count // SHORT
    heads = width // HEAD
    hidden = n.we.shape[1]
    me = lax.axis_index("mp")
    core = me + 1 - 2 * lax.rem(me, 2)
    across = lax.rem(me + parts // 2, parts)
    corner = lax.rem(core + parts // 2, parts)
    side = lax.rem(me, 2)
    peers = (core, across, corner)
    dp = lax.axis_index("dp")

    loads = [
        pltpu.make_async_copy(src, dst, n.load_s.at[0, k])
        for k, (src, dst) in enumerate(
            ((n.res, n.Q), (n.cot, n.K), (n.wo, n.WO.at[at(me, width)]), (n.we, n.WE), (n.wr, n.WR))
        )
    ]
    for c in loads:
        c.start()
    barrier = pltpu.get_barrier_semaphore()
    for peer in peers:
        pl.semaphore_signal(barrier, inc=1, device_id={"mp": peer}, device_id_type=MESH)

    def each_group(body):
        def run(d, _):
            body(d, lax.rem(dp + d, groups))
            return 0

        lax.fori_loop(1, groups, run, 0)

    each_group(
        lambda d, group: pl.semaphore_signal(
            barrier, inc=1, device_id={"dp": group}, device_id_type=MESH
        )
    )
    pl.semaphore_wait(barrier, len(peers) + groups - 1)
    feed = Reduce(n.BM, n.BM1, n.BM2, n.BM3, (n.bm_s, n.bm_r), dp, groups)
    spare = (n.WE.at[:, : 2 * width], n.WE.at[:, 2 * width :], n.WR.at[:, : 2 * width])
    rest = Reduce(n.BT, *spare, (n.bt_s, n.bt_r), dp, groups)

    def gather(buf, sems):
        return Gather(
            lambda slot, i: buf.at[slot, at(i, PACKED)], sems, me, core, across
        )

    res = gather(n.RES, (n.res_s, n.res_r))
    cot = gather(n.COT, (n.cot_s, n.cot_r))
    mix = gather(n.MIX, (n.mix_s, n.mix_r))
    weight = Gather(lambda slot, i: n.WO.at[at(slot, width)], (n.wo__s, n.wo__r), me, core, across)

    def vec_copy(k):
        return copy_to(n.VEC.at[me], n.VEC.at[me], n.vec__s.at[k, 0], n.vec__r.at[k, 0], peers[k])

    def join(buf, i):
        pieces = [unpack(buf[p, at(i, PACKED)]) for p in range(parts)]
        return jnp.concatenate(pieces, axis=1)

    def own_columns(ref_write, values):
        for p in range(parts):

            @pl.when(me == p)
            def _():
                ref_write(values[:, p * width : (p + 1) * width])

    n.VEC[me] = n.vec[...]
    for k in range(3):
        vec_copy(k).start()
    for c in loads[:1]:
        c.wait()
    for i in range(blocks):
        n.RES[me, i * PACKED : (i + 1) * PACKED] = pack(n.Q[i * SHORT : (i + 1) * SHORT])
        res.start(i)
    for c in loads[1:]:
        c.wait()
    for i in range(blocks):
        n.COT[me, i * PACKED : (i + 1) * PACKED] = pack(n.K[i * SHORT : (i + 1) * SHORT])
    for ref in (n.GWE, n.GWR, n.DV, n.ACC, n.GB):
        ref[...] = jnp.zeros_like(ref)
    total = n.lengths[0, 0]
    for slot in range(1, n.lengths.shape[1]):
        total = total + n.lengths[0, slot]
    far = jnp.where(n.lengths[0, 0] == LONG, 0.0, FAR)
    for k in range(3):
        vec_copy(k).wait_recv()
    for row in range(4):
        n.GAINS[row : row + 1] = jnp.concatenate(
            [n.VEC[p, row : row + 1, :width] for p in range(parts)], axis=1
        )

    def forward_block(i, _):
        res.forward(i)

        @pl.when(i == 1)
        def _():
            weight.start(0)

        @pl.when(i >= 2)
        def _():
            cot.start(2 * i - 4)
            cot.start(2 * i - 3)

        res.finish(i)
        here = at(i, SHORT)
        full, inverse = decompress(join(n.RES, i).astype(F32))
        rows = (full * inverse * n.GAINS[0:1]).astype(BF16)
        q = (dot(rows, n.w[0]) + n.bias[0:1]).astype(BF16)
        k = dot(rows, n.w[1]).astype(BF16)
        v = (dot(rows, n.w[2]) + n.bias[1:2]).astype(BF16)
        v = jnp.concatenate([v, jnp.ones((SHORT, HEAD), BF16)], axis=1)
        n.Q[here] = q
        n.K[here] = k
        n.VX[here] = v
        live = i * SHORT < total
        allowed = diagonal(live, False)
        scaled = q * SCORE_SCALE
        q_heads = [head_of(scaled, h) for h in range(heads)]
        carry = []
        for h in range(heads):
            s = jnp.where(allowed, dot_nt(q_heads[h], k), -FAR)
            m = jnp.max(s, axis=1, keepdims=True)
            carry.append((m, dot(jnp.exp(s - m).astype(BF16), v)))

        def body(j, carry):
            k_j = n.K[at(j, SHORT)]
            v_j = n.VX[at(j, SHORT)]
            after = []
            for h in range(heads):
                m, acc = carry[h]
                s = dot_nt(q_heads[h], k_j)
                new = jnp.maximum(m, jnp.max(s, axis=1, keepdims=True) - far)
                p = jnp.exp(s - (new + far)).astype(BF16)
                after.append((new, acc * jnp.exp(m - new) + dot(p, v_j)))
            return after

        carry = lax.fori_loop(0, i, body, carry)
        mixed = jnp.zeros((SHORT, width), F32)
        lse = jnp.zeros((SHORT, LANES), F32)
        for h in range(heads):
            m, acc = carry[h]
            norm = acc[:, width : width + 1]
            mixed = mixed + head_of(acc[:, :width] / norm, h)
            lse = jnp.where(lanes(lse.shape) == h, m + jnp.log(norm), lse)
        n.LSE[i] = jnp.transpose(lse)[:8]
        n.MIX[me, at(i, PACKED)] = pack(mixed.astype(BF16))
        mix.start(i)

        @pl.when(i >= 1)
        def _():
            mix.forward(i - 1)

        return 0

    lax.fori_loop(0, blocks, forward_block, 0)

    def e2_half(i, which):
        return n.E2P.at[pl.ds(pl.multiple_of(i * SHORT + which * HALF, HALF), HALF)]

    def e2_first(i):
        return copy_to(e2_half(i, 1 - side), n.E2C.at[i], n.e2a_s.at[0, i], n.e2a_r.at[0, i], core)

    def e2_cross(i):
        return copy_to(n.E2C.at[i], n.E2Y.at[i], n.e2x_s.at[0, i], n.e2x_r.at[0, i], across)

    def e2_last(i):
        return copy_to(e2_half(i, side), n.E2T.at[i], n.e2b_s.at[0, i], n.e2b_r.at[0, i], core)

    def e2_sum(i):
        e2_first(i).wait_recv()
        own = n.E2P[pl.ds(pl.multiple_of(i * SHORT + side * HALF, HALF), HALF)].astype(F32)
        n.E2C[i] = (own + n.E2C[i].astype(F32)).astype(BF16)
        e2_cross(i).start()

    def e2_total(i):
        e2_cross(i).wait_recv()
        both = n.E2C[i].astype(F32) + n.E2Y[i].astype(F32)
        n.E2P[pl.ds(pl.multiple_of(i * SHORT + side * HALF, HALF), HALF)] = both.astype(BF16)
        e2_last(i).start()

    def scatter_first(P, C, sems, slot, i):
        targets = (core, corner)
        return [
            copy_to(P.at[slot, targets[k]], C.at[k, i], sems[0].at[k, i], sems[1].at[k, i], core)
            for k in range(2)
        ]

    def scatter_sum(P, C, first, slot, i):
        for c in first:
            c.wait_recv()
        for k, owner in enumerate((me, across)):
            C[k, i] = (P[slot, owner].astype(F32) + C[k, i].astype(F32)).astype(BF16)

    def scatter_cross(C, Y, sems, i):
        return copy_to(C.at[1, i], Y.at[i], sems[0].at[0, i], sems[1].at[0, i], across)

    b2_sems, b2x_sems = (n.b2c_s, n.b2c_r), (n.b2x_s, n.b2x_r)
    e1_sems, e1x_sems = (n.e1c_s, n.e1c_r), (n.e1x_s, n.e1x_r)

    def b2_first(slot, i):
        return scatter_first(n.PIECES, n.B2C, b2_sems, slot, i)

    def b2_cross(i):
        return scatter_cross(n.B2C, n.B2Y, b2x_sems, i)

    def e1_first(slot, i):
        return scatter_first(n.PIECES, n.E1C, e1_sems, slot, i)

    def e1_cross(i):
        return scatter_cross(n.E1C, n.E1Y, e1x_sems, i)

    def split(P, slot, values):
        for p in range(parts):
            P[slot, p] = pack(values[:, p * width : (p + 1) * width])

    def order(step):
        return lax.rem(blocks - step, blocks)

    weight.forward(0)
    cot.forward(0)
    cot.forward(1)
    weight.finish(0)

    def add_thirds(ref, values):
        for c in range(3):
            ref[c * D : (c + 1) * D] += values[:, c * 2 * LANES : (c + 1) * 2 * LANES]

    def middle_block(step, _):
        i = order(step)
        slot = lax.rem(step, 2)

        @pl.when(step == 1)
        def _():
            mix.forward(blocks - 1)
            cot.forward(2)
            cot.forward(3)

        mix.finish(i)
        cot.finish(i)
        here = at(i, SHORT)
        full, _unused = decompress(join(n.RES, i).astype(F32))
        x1 = full + center(dot(join(n.MIX, i), n.WO[...]) + n.GAINS[1:2])
        n.X1[here] = x1
        rows = (x1 * inverse_rms(x1) * n.GAINS[2:3]).astype(BF16)
        z = dot(rows, n.WE[...]) + n.be[...]
        t = jnp.tanh(0.7978845608 * (z + 0.044715 * (z * z * z)))
        active = (0.5 * z * (1.0 + t)).astype(BF16)
        slope = 0.5 * (1.0 + t) + 0.5 * z * (1.0 - t * t) * (
            0.7978845608 * (1.0 + (3 * 0.044715) * (z * z))
        )
        slope = slope.astype(BF16)

        @pl.when(step >= 2)
        def _():
            e2_sum(order(step - 1))

        @pl.when(step >= 1)
        def _():
            before = order(step - 1)
            scatter_sum(n.PIECES, n.B2C, b2_first(1 - slot, before), 1 - slot, before)

        @pl.when(step >= 2)
        def _():
            for c in b2_first(slot, order(step - 2)):
                c.wait_send()

        split(n.PIECES, slot, center(dot(active, n.WR[...])).astype(BF16))
        for c in b2_first(slot, i):
            c.start()
        g2 = branch_grad(join(n.COT, i).astype(F32))
        n.ACC[0:1] += jnp.sum(g2, axis=0, keepdims=True)
        g2 = g2.astype(BF16)
        add_thirds(n.GWR, dot_tn(active, g2))
        d_hidden = (dot_nt(g2, n.WR[...]) * slope).astype(BF16)
        n.ACC[1:2, :hidden] += jnp.sum(d_hidden.astype(F32), axis=0, keepdims=True)
        add_thirds(n.GWE, dot_tn(rows, d_hidden))
        n.E2P[here] = dot_nt(d_hidden, n.WE[...]).astype(BF16)
        e2_first(i).start()
        return 0

    lax.fori_loop(0, blocks, middle_block, 0)
    last = (blocks - 1) % 2
    e2_sum(order(blocks - 1))
    e2_sum(0)
    scatter_sum(n.PIECES, n.B2C, b2_first(last, order(blocks - 1)), last, order(blocks - 1))
    for c in range(3):
        block = slice(c * 2 * LANES, (c + 1) * 2 * LANES)
        n.BM[:D, block] = n.GWE[c * D : (c + 1) * D].astype(BF16)
        n.BM[D:, block] = n.GWR[c * D : (c + 1) * D].astype(BF16)
    feed.start()

    for slot, step in ((1 - last, blocks - 2), (last, blocks - 1)):
        for c in b2_first(slot, order(step)):
            c.wait_send()
    n.GWE[...] = jnp.zeros_like(n.GWE)
    n.GWR[...] = jnp.zeros_like(n.GWR)

    x1_own, tokens = 2 * LANES, 4 * LANES

    def stat_copy(k, i):
        mine = n.STAT.at[me, i]
        return copy_to(mine, mine, n.stat_s.at[k, i], n.stat_r.at[k, i], peers[k])

    columns = me * width + lanes((1, width))
    stored = columns < D - 1

    def finish_grad(i):
        here = at(i, SHORT)
        e1_cross(i).wait_recv()
        for k in range(3):
            stat_copy(k, i).wait_recv()
        stat = jnp.zeros((8, SHORT), F32)
        for p in range(parts):
            stat = stat + n.STAT[p, i]
        stat = jnp.transpose(jnp.concatenate([stat] * (LANES // 8), axis=0))
        along, c_last = stat[:, 0:1], stat[:, 1:2]

        @pl.when(i == 0)
        def _():
            n.GB[4:5] = jnp.zeros((1, width), F32) + jnp.sum(
                sum(n.STAT[p, i, 2:3] for p in range(parts)), axis=1, keepdims=True
            )

        tok = n.X1[here, tokens : tokens + LANES]
        inverse, u_last, g_last = tok[:, 0:1], tok[:, 1:2], tok[:, 2:3]
        e1 = unpack(n.E1C[0, i].astype(F32) + n.E1Y[i].astype(F32))
        u_own = jnp.where(stored, unpack(n.RES[me, at(i, PACKED)]).astype(F32), u_last)
        n.GB[2:3] += jnp.sum(e1 * u_own * inverse, axis=0, keepdims=True)
        cube = inverse * inverse * inverse * along / D
        own = n.X1[here, :width] + inverse * (e1 * n.vec[0:1, :width]) - u_own * cube
        final = g_last + inverse * c_last - u_last * cube
        n.Q[here] = jnp.where(stored, own - final, 0.0).astype(BF16)

    def finish_out(i):
        here = at(i, SHORT)
        b2_cross(i).wait_recv()
        b2 = unpack(n.B2C[0, i].astype(F32) + n.B2Y[i].astype(F32))
        bias = n.vec[3:4, :width] - jnp.mean(n.GAINS[3:4], axis=1, keepdims=True)
        live = (i * SHORT + rows_of((SHORT, 1))) < total

        x2 = n.X1[here, x1_own : x1_own + width] + b2 + bias
        n.K[here] = jnp.where(stored, x2, 0.0).astype(BF16)
        n.GB[3:4] += jnp.sum(jnp.where(live, x2 * x2, 0.0), axis=0, keepdims=True)

    def backward_block(step, _):
        i = blocks - 1 - step
        slot = lax.rem(step, 2)
        here = at(i, SHORT)

        @pl.when(step == 0)
        def _():
            e2_total(i)

        @pl.when(step == 1)
        def _():
            for b in range(blocks):
                b2_cross(b).start()

        e2_last(i).wait_recv()
        e2_first(i).wait_send()
        n.E2P[pl.ds(pl.multiple_of(i * SHORT + (1 - side) * HALF, HALF), HALF)] = n.E2T[i]
        x1 = n.X1[here]
        inverse = inverse_rms(x1)
        e2 = n.E2P[here].astype(F32)
        n.ACC[2:3] += jnp.sum(e2 * x1 * inverse, axis=0, keepdims=True)
        c = e2 * n.GAINS[2:3]
        along = jnp.sum(c * x1, axis=1, keepdims=True)
        du = inverse * c - x1 * (inverse * inverse * inverse * along / D)
        g1 = branch_grad(join(n.COT, i).astype(F32)) + center(du)
        n.ACC[3:4] += jnp.sum(g1, axis=0, keepdims=True)
        g1_last = g1[:, D - 1 :]

        for p in range(parts):

            @pl.when(me == p)
            def _():
                n.X1[here, :width] = g1[:, p * width : (p + 1) * width]
                n.X1[here, x1_own : x1_own + width] = x1[:, p * width : (p + 1) * width]

        g1 = g1.astype(BF16)
        mixed = unpack(n.MIX[me, at(i, PACKED)])
        g_output = dot_tn(g1, mixed)
        for h in range(heads):
            n.GWE[h * D : (h + 1) * D, width:] += g_output[:, h * HEAD : (h + 1) * HEAD]
        d_mixed = dot_nt(g1, n.WO[at(me, width)]).astype(BF16)
        product = d_mixed.astype(F32) * mixed.astype(F32)
        product = jnp.transpose(jnp.concatenate([product, jnp.zeros((SHORT, HEAD), F32)], axis=1))
        delta = [
            jnp.sum(product[h * HEAD : (h + 1) * HEAD], axis=0, keepdims=True)
            for h in range(heads)
        ]
        lse = [n.LSE[i, h : h + 1] for h in range(heads)]
        live = i * SHORT < total
        scaled = n.Q[here] * SCORE_SCALE
        q_heads = [head_of(scaled, h) for h in range(heads)]
        g_heads = [head_of(d_mixed, h) for h in range(heads)]
        def pair(there, lse, allowed):
            k_j = n.K[there]
            v_j = n.VX[there][:, :width]
            k_scaled = k_j * SCORE_SCALE
            dk = dv = dq = jnp.zeros((SHORT, width), F32)
            for h in range(heads):
                p = jnp.exp(dot_nt(k_j, q_heads[h]) - lse[h])
                if allowed is not None:
                    p = jnp.where(allowed, p, 0.0)
                dv = dv + dot(p.astype(BF16), g_heads[h])
                p = (p * (dot_nt(v_j, g_heads[h]) - delta[h])).astype(BF16)
                dk = dk + dot(p, q_heads[h])
                dq = dq + dot_tn(p, head_of(k_scaled, h))
            n.DV[there] += dv
            n.GWR[there, :width] += dk
            return dq

        dq = pair(here, lse, diagonal(live, True))

        @pl.when(i >= 1)
        def _():
            e2_total(i - 1)

        @pl.when(step == 1)
        def _():
            feed.sum_quarter(3)

        @pl.when(step == 2)
        def _():
            feed.sum_owners()

        @pl.when(step == blocks - 1)
        def _():
            for b in range(blocks):
                finish_out(b)

        @pl.when(step >= 1)
        def _():
            scatter_sum(n.PIECES, n.E1C, e1_first(1 - slot, i + 1), 1 - slot, i + 1)
            e1_cross(i + 1).start()

        lse_far = [row + far for row in lse]

        def body(j, dq):
            dq = dq + pair(at(j, SHORT), lse_far, None)

            @pl.when(step == 0)
            def _():
                feed.sum_quarter(j)

            return dq

        dq = lax.fori_loop(0, i, body, dq).astype(BF16)
        dk = n.GWR[here, :width].astype(BF16)
        dv = n.DV[here].astype(BF16)
        n.GB[0:1] += jnp.sum(dq.astype(F32), axis=0, keepdims=True)
        n.GB[1:2] += jnp.sum(dv.astype(F32), axis=0, keepdims=True)
        full, inverse = decompress(join(n.RES, i).astype(F32))
        rows = (full * inverse * n.GAINS[0:1]).astype(BF16)
        e1 = jnp.zeros((SHORT, D), F32)
        for c, d in enumerate((dq, dk, dv)):
            n.GWE[c * D : (c + 1) * D, :width] += dot_tn(rows, d)
            e1 = e1 + dot_nt(d, n.w[c])

        @pl.when(step >= 2)
        def _():
            for c in e1_first(slot, i + 2):
                c.wait_send()

        split(n.PIECES, slot, e1.astype(BF16))
        for c in e1_first(slot, i):
            c.start()
        c = e1 * n.GAINS[0:1]
        lane = lanes((SHORT, LANES))
        stat = jnp.where(lane == 0, jnp.sum(c * full, axis=1, keepdims=True), 0.0)
        stat = jnp.where(lane == 1, c[:, D - 1 :], stat)
        n.STAT[me, i] = jnp.transpose(stat)[:8]
        n.STAT[me, i, 2:3, :width] = n.GB[3:4]
        for k in range(3):
            stat_copy(k, i).start()
        tok = jnp.where(lane == 0, inverse, 0.0)
        tok = jnp.where(lane == 1, full[:, D - 1 :], tok)
        n.X1[here, tokens : tokens + LANES] = jnp.where(lane == 2, g1_last, tok)

        @pl.when(step >= 2)
        def _():
            finish_grad(i + 2)

        return 0

    lax.fori_loop(0, blocks, backward_block, 0)
    scatter_sum(n.PIECES, n.E1C, e1_first(last, 0), last, 0)
    e1_cross(0).start()

    for c in range(3):
        n.BT[c // 2 * D : c // 2 * D + D, c % 2 * width : c % 2 * width + width] = n.GWE[
            c * D : (c + 1) * D, :width
        ].astype(BF16)
    n.BT[D:, width:] = jnp.concatenate(
        [n.GWE[h * D : (h + 1) * D, width:] for h in range(heads)], axis=1
    ).astype(BF16)
    rest.start()
    finish_grad(1)
    feed.forward()
    rest.sum_quarter(0)
    rest.sum_quarter(1)
    finish_grad(0)
    rest.sum_quarter(2)
    rest.sum_quarter(3)

    def tiny_copy(slot, group):
        here = n.SMALL.at[dp]
        return pltpu.make_async_remote_copy(
            src_ref=here,
            dst_ref=here,
            send_sem=n.tiny_s.at[0, group],
            recv_sem=n.tiny_r.at[0, slot],
            device_id={"dp": group},
            device_id_type=MESH,
        )

    n.SMALL[dp] = jnp.zeros((16, 2 * LANES), F32)
    n.SMALL[dp, 0:3, :width] = n.GB[0:3]
    n.SMALL[dp, 3:4, :width] = n.GB[4:5]
    n.SMALL[dp, 7:8] = jnp.zeros((1, 2 * LANES), F32) + total.astype(F32)
    for row, source in ((4, 3), (5, 2), (6, 0)):

        def write_small(values, row=row):
            n.SMALL[dp, row : row + 1, :width] = values

        own_columns(write_small, n.ACC[source : source + 1])
    for p in range(parts):
        n.SMALL[dp, 8 + p : 9 + p, :width] = n.ACC[1:2, p * width : (p + 1) * width]
    each_group(lambda d, group: tiny_copy(dp, group).start())

    def store(src, dst, k):
        return pltpu.make_async_copy(src, dst, n.store_s.at[0, k])

    stores = [store(n.Q, n.grad, 0), store(n.K, n.out, 1)]
    for c in stores:
        c.start()
    rest.sum_owners()
    feed.finish()

    def store_feed(half, rows):
        target, k = ((n.gwe, 2), (n.gwr, 3))[half]
        stage = n.X1.at[half * D : (half + 1) * D]
        stage[...] = rows[...].astype(F32)
        store(stage, target, k).start()

    feed.take(store_feed)
    stores += [store(n.X1.at[:D], n.gwe, 2), store(n.X1.at[D : 2 * D], n.gwr, 3)]
    rest.forward()
    each_group(lambda d, group: tiny_copy(group, group).wait_recv())
    small = n.SMALL[0]
    for group in range(1, groups):
        small = small + n.SMALL[group]
    n.small[...] = small
    rest.finish()

    def store_rest(half, rows):
        if half == 0:
            n.DV[:D] = rows[:, :width].astype(F32)
            n.DV[D : 2 * D] = rows[:, width:].astype(F32)
            store(n.DV.at[:D], n.gw.at[0], 4).start()
            store(n.DV.at[D : 2 * D], n.gw.at[1], 5).start()
        else:
            n.DV[2 * D :] = rows[:, :width].astype(F32)
            store(n.DV.at[2 * D :], n.gw.at[2], 6).start()
            n.X1[2 * D : 2 * D + width] = jnp.transpose(rows[:, width:].astype(F32))
            store(n.X1.at[2 * D : 2 * D + width], n.gwo, 7).start()

    rest.take(store_rest)
    stores += [
        store(n.DV.at[:D], n.gw.at[0], 4),
        store(n.DV.at[D : 2 * D], n.gw.at[1], 5),
        store(n.DV.at[2 * D :], n.gw.at[2], 6),
        store(n.X1.at[2 * D : 2 * D + width], n.gwo, 7),
    ]

    for k in range(3):
        vec_copy(k).wait_send()
    weight.drain(0)

    def drain(i, _):
        for g in (res, cot, mix):
            g.drain(i)
        for c in (e2_cross, e2_last, b2_cross, e1_cross):
            c(i).wait_send()
        for k in range(3):
            stat_copy(k, i).wait_send()
        return 0

    lax.fori_loop(0, blocks, drain, 0)
    for step in (blocks - 2, blocks - 1):
        for c in e1_first(step % 2, blocks - 1 - step):
            c.wait_send()
    for c in stores:
        c.wait()
    feed.drain()
    rest.drain()
    each_group(lambda d, group: tiny_copy(dp, group).wait_send())


def on_device(
    residual,
    lengths,
    gain_one,
    input_weight,
    input_bias,
    output_weight,
    output_bias,
    gain_two,
    expand_weight,
    expand_bias,
    reduce_weight,
    reduce_bias,
    cotangent,
):
    count, width = residual.shape
    hidden = expand_weight.shape[1]

    def shape(*dims, dtype=BF16):
        return jax.ShapeDtypeStruct(dims, dtype)

    vec = jnp.stack([gain_one, output_bias, gain_two, reduce_bias])
    vec = jnp.pad(vec, ((0, 4), (0, 2 * LANES - width)))
    groups = lax.axis_size("dp")
    names, scratches = scratch(count, width, hidden, groups)
    vmem = pl.BlockSpec(memory_space=pltpu.VMEM)
    hbm = pl.BlockSpec(memory_space=pl.ANY)
    out, grad, gw, gwo, gwe, gwr, small = pl.pallas_call(
        lambda *refs: layer_kernel(groups, names, *refs),
        in_specs=[pl.BlockSpec(memory_space=pltpu.SMEM)]
        + [hbm if name in IN_HBM else vmem for name in INPUTS[1:]],
        out_specs=[hbm if name in IN_HBM else vmem for name in OUTPUTS],
        out_shape=[
            shape(count, width),
            shape(count, width),
            shape(3, D, width, dtype=F32),
            shape(width, D, dtype=F32),
            shape(D, hidden, dtype=F32),
            shape(hidden, D, dtype=F32),
            shape(16, 2 * LANES, dtype=F32),
        ],
        scratch_shapes=scratches,
        compiler_params=pltpu.CompilerParams(
            vmem_limit_bytes=63 << 20, collective_id=0, has_side_effects=True
        ),
        name="layer",
    )(
        lengths, residual, cotangent, vec, input_weight, input_bias, output_weight,
        expand_weight, expand_bias[None], reduce_weight,
    )

    small = small[:, :width]
    live_count = small[7, 0].astype(jnp.int32)
    residual_rms = jnp.sqrt(small[3, 0] / (D * small[7, 0]))
    return (
        out,
        grad,
        gw,
        small[0:2],
        gwo,
        small[4],
        small[2],
        small[5],
        gwe,
        small[8:12].reshape(hidden),
        gwr,
        small[6],
        residual_rms,
        live_count,
    )


def solution(mesh):
    return jax.shard_map(
        on_device,
        mesh=mesh,
        in_specs=(
            P("dp", "mp"),
            P("dp", None),
            P("mp"),
            P(None, None, "mp"),
            P(None, "mp"),
            P("mp", None),
            P("mp"),
            P("mp"),
            P(None, "mp"),
            P("mp"),
            P("mp", None),
            P("mp"),
            P("dp", "mp"),
        ),
        out_specs=(
            P("dp", "mp"),
            P("dp", "mp"),
            P(None, None, "mp"),
            P(None, "mp"),
            P("mp", None),
            P("mp"),
            P("mp"),
            P("mp"),
            P(None, "mp"),
            P("mp"),
            P("mp", None),
            P("mp"),
            P(),
            P(),
        ),
        check_vma=False,
    )
```

time: 631 us -> 241 us (0.38)
  waiting for transfers between devices: 357 us -> 0 us
  Pallas kernels: 103 us -> 208 us
  blocking collectives: 88.7 us -> 0 us
  local copies, waits for them, and re-layouts: 45.4 us -> 22.9 us
  other arithmetic: 15.9 us -> 1.34 us
  between operations: 17.9 us -> 4.94 us
    psum x3 -> x0, waiting for transfers between devices: 223 us -> none  [the longest x1 79.3 us: on_device(): gwe, gwr = lax.psum((gwe, gwr), 'dp')]
    pallas_call x3 -> x1, Pallas kernels: 103 us -> 208 us  [on_device(): pl.pallas_call(lambda *refs: layer_kernel(groups, names, *refs), in_specs...]
    psum x4 -> x0, blocking collectives: 82.6 us -> none  [the longest x1 37.1 us: on_device(): square = lax.psum(square, ('dp', 'mp'))]
    unnamed x11 -> x0, waiting for transfers between devices: 75.4 us -> none
    all_gather x4 -> x0, waiting for transfers between devices: 59.3 us -> none  [the longest x1 22.6 us: on_device(): mixed_full = lax.all_gather(mixed, 'mp', axis=1, tiled=True)]
    all_gather x4 -> x0, local copies, waits for them, and re-layouts: 14.1 us -> none  [the longest x1 4.73 us: on_device(): res_full = lax.all_gather(residual, 'mp', axis=1, tiled=True)]
    reduce_sum x3 -> x0, other arithmetic: 7.31 us -> none  [the longest x1 5.48 us: on_device(): square = jnp.sum(jnp.where(live[:, None], x2 * x2, 0.0))]
    unnamed x40 -> x21, local copies, waits for them, and re-layouts: 21.2 us -> 16.2 us
  transfers between devices with their start and end apart: 9 -> 0, of which waited for: 8 -> 0; matrix products, arithmetic and copies ran while one was open for 7% -> 0% of each run, Pallas kernels for 4% -> 0%
where the time goes in v2:
time: 241 us; the launch traced here: 237 us
  Pallas kernels  208 us (86%)
  local copies, waits for them, and re-layouts  22.9 us (10%)
  between operations  4.94 us (2%)
    pallas_call x1, Pallas kernels, on_device(): pl.pallas_call(lambda *refs: layer_kernel(groups, names, *refs), in_specs...  208 us
    unnamed x21, local copies, waits for them, and re-layouts  16.2 us

profile of v2, /device:TPU:0, one launch (start us, length us, event | category | flops | bytes accessed | tf_op | source)
XLA Modules:
  0.0 236.9 jit_solution(4259246310550957933)
XLA Ops:
  0.6 0.0 copy-start.4
  0.7 0.0 copy-start.3
  0.7 1.4 broadcast_in_dim.3.refs_8_
  2.1 1.3 select_maximum_fusion.refs_3_
  3.4 2.2 copy.27.refs_1_
  5.6 0.0 copy-done.4
  5.6 1.3 copy.28.refs_2_
  6.9 0.0 copy-done.3
  6.9 1.4 copy.29.refs_4_
  8.3 207.7 %layer.1 = (bf16[2048,192]{1,0:T(8,128)(2,1)}, bf16[2048,192]{1,0:T(8,128)(2,1)}, f32[3,768,192]{2,1,0:T(8,128)}, f32[192,768]{1,0:T(8,128)}, f32[768,768]{1,0:T...) custom-call(s32[1,4]{1,0:T(1,128)} %refs_0_.1, bf16[2048,192]{1,0:T(8,128)(2,1)} %copy.27.refs_1_, ...), custom_call_target="tpu_custom_call" | custom-call | tf_op jit(solution)/shard_map/layer/pallas_call | solution.py:939
  216.0 0.0 copy-start.2
  216.0 2.3 copy.30
  218.3 1.3 fusion
  221.6 1.3 slice.34
  222.9 0.7 slice.38
  223.6 1.4 fusion.1
  225.0 0.7 reshape.36
  225.6 1.2 copy.31
  226.9 3.1 %copy.32 = f32[3,768,192]{1,2,0:T(8,128)} copy(f32[3,768,192]{2,1,0:T(8,128)} %get-tuple-element.30) | data formatting | bytes 3538944
  229.9 0.0 copy-done.5
  229.9 0.8 copy.36
  230.8 1.4 copy.37
  232.2 1.1 copy-done
  233.3 1.4 copy.38
  (5 shorter events, 0.0 us)
Async XLA Ops:
  0.6 5.0 %copy-start.4 = (bf16[2048,192]{0,1:T(8,128)(2,1)S(1)}, bf16[2048,192]{0,1:T(8,128)(2,1)}, u32[]{:S(2)}) copy-start(bf16[2048,192]{0,1:T(8,128)(2,1)} %param.25) | copy-start | bytes 2359300
  0.7 6.2 %copy-start.3 = (bf16[3,768,192]{1,2,0:T(8,128)(2,1)S(1)}, bf16[3,768,192]{1,2,0:T(8,128)(2,1)}, u32[]{:S(2)}) copy-start(bf16[3,768,192]{1,2,0:T(8,128)(2,1)} %param.16) | copy-start | bytes 2654212
  216.0 9.6 %copy-start.2 = (bf16[2048,192]{1,0:T(8,128)(2,1)S(1)}, bf16[2048,192]{1,0:T(8,128)(2,1)}, u32[]{:S(2)}) copy-start(bf16[2048,192]{1,0:T(8,128)(2,1)} %get-tuple-element.29) | copy-start | bytes 2359300
  226.9 3.1 %copy-start.5 = (f32[192,768]{1,0:T(8,128)S(1)}, f32[192,768]{1,0:T(8,128)}, u32[]{:S(2)}) copy-start(f32[192,768]{1,0:T(8,128)} %get-tuple-element.66) | copy-start | bytes 1769476
  226.9 3.9 %copy-start.1 = (f32[768,768]{1,0:T(8,128)S(1)}, f32[768,768]{1,0:T(8,128)}, u32[]{:S(2)}) copy-start(f32[768,768]{1,0:T(8,128)} %get-tuple-element.70) | copy-start | bytes 7077892
  230.8 2.5 %copy-start = (f32[768,768]{1,0:T(8,128)S(1)}, f32[768,768]{1,0:T(8,128)}, u32[]{:S(2)}) copy-start(f32[768,768]{1,0:T(8,128)} %get-tuple-element.72) | copy-start | bytes 7077892

commit v3 on v2

v3 whole, which is shorter than its diff:
```python
import types

import jax
import jax.numpy as jnp
from jax import lax
from jax.experimental import pallas as pl
from jax.experimental.pallas import tpu as pltpu
from jax.sharding import PartitionSpec as P


D = 768
HEAD = 64
SHORT = 512
LONG = 2048
EPSILON = 1e-05
SCORE_SCALE = 0.125
FAR = 1e30
LANES = 128
SUBLANES = 8
MESH = pl.DeviceIdType.MESH

F32 = jnp.float32
BF16 = jnp.bfloat16
NT = (((1,), (1,)), ((), ()))


def dot(a, b):
    return jnp.dot(a, b, preferred_element_type=F32)


def dot_nt(a, b):
    return lax.dot_general(a, b, NT, preferred_element_type=F32)


def lanes(shape):
    return lax.broadcasted_iota(jnp.int32, shape, 1)


def rows_of(shape):
    return lax.broadcasted_iota(jnp.int32, shape, 0)


def at(index, size):
    return pl.ds(pl.multiple_of(index * size, size), size)


def column_sum(values):
    return jnp.sum(values, axis=0, keepdims=True)


def with_last(values, last):
    cut = values.shape[0] - SUBLANES
    end = values[cut:]
    end = jnp.where(rows_of(end.shape) == SUBLANES - 1, last, end)
    return jnp.concatenate([values[:cut], end], axis=0)


def decompress(raw):
    full = with_last(raw, 0.0)
    full = with_last(full, -column_sum(full))
    return full, inverse_rms(full)


def inverse_rms(full):
    return lax.rsqrt(column_sum(full * full) / D + EPSILON)


def center(values):
    return values - column_sum(values) / D


def branch_grad(raw):
    return center(with_last(raw, 0.0))


def diagonal(live):
    key = rows_of((SHORT, SHORT))
    query = lanes((SHORT, SHORT))
    return (key == query) | ((key < query) & live)


def pick(lane):
    return (lanes((SHORT, LANES)) == lane).astype(BF16)


def copy_to(src, dst, send_sem, recv_sem, peer):
    return pltpu.make_async_remote_copy(
        src_ref=src,
        dst_ref=dst,
        send_sem=send_sem,
        recv_sem=recv_sem,
        device_id={"mp": peer},
        device_id_type=MESH,
    )


class Gather:
    def __init__(self, piece, source, sems, me, core, across):
        self.piece, self.source = piece, source
        self.me, self.core, self.across = me, core, across
        self.send, self.recv = sems

    def copy(self, kind, i):
        slot = self.across if kind == 2 else self.me
        peer = self.across if kind == 1 else self.core
        there = self.piece(slot, i)
        here = there if kind == 2 else self.source(i)
        return copy_to(here, there, self.send.at[kind, i], self.recv.at[kind, i], peer)

    def start(self, i):
        self.copy(1, i).start()
        self.copy(0, i).start()

    def forward(self, i):
        self.copy(1, i).wait_recv()
        self.copy(2, i).start()

    def finish(self, i):
        self.copy(0, i).wait_recv()
        self.copy(2, i).wait_recv()

    def drain(self, i):
        for kind in range(3):
            self.copy(kind, i).wait_send()


INPUTS = ("lengths", "res", "cot", "vec", "w", "wo", "we", "wr")
OUTPUTS = ("out", "grad", "rest", "feed", "small")
IN_VMEM = ("vec", "small")


class Reduce:
    def __init__(self, buf, first, second, other, sems, dp, size):
        self.buf, self.first, self.second, self.other = buf, first, second, other
        self.sems = sems
        self.high = buf.shape[0] // 2
        self.count = size // 2
        self.piece = self.high // self.count
        self.side = lax.rem(dp, 2)
        self.place = lax.div(dp, 2)
        self.mate = dp + 1 - 2 * self.side

    def rows(self, p, base=0):
        return pl.ds(pl.multiple_of(base + p * self.piece, self.piece), self.piece)

    def own(self, p):
        return self.buf.at[self.rows(p, self.side * self.high)]

    def copy(self, src, dst, stage, p, slot, peer):
        return pltpu.make_async_remote_copy(
            src_ref=src,
            dst_ref=dst,
            send_sem=self.sems[0].at[stage, p],
            recv_sem=self.sems[1].at[stage, slot],
            device_id={"dp": peer},
            device_id_type=MESH,
        )

    def to_mate(self, p):
        away = self.buf.at[self.rows(p, (1 - self.side) * self.high)]
        return self.copy(away, self.first.at[self.rows(p)], 0, p, p, self.mate)

    def to_owner(self, p, slot):
        return self.copy(
            self.first.at[self.rows(p)], self.second.at[self.rows(slot)], 1, p, slot, 2 * p + self.side
        )

    def to_peer(self, p, slot):
        return self.copy(self.own(slot), self.own(slot), 2, p, slot, 2 * p + self.side)

    def back(self, p):
        return self.copy(self.own(p), self.other.at[self.rows(p)], 3, p, p, self.mate)

    def each(self, body, start=0, stop=None):
        def run(p, _):
            body(p)
            return 0

        lax.fori_loop(start, self.count if stop is None else stop, run, 0)

    def others(self, body):
        def run(p):
            @pl.when(p != self.place)
            def _():
                body(p)

        self.each(run)

    def turn(self, k):
        half = self.count // 2
        return lax.rem(k, 2) * half + lax.div(k, 2)

    def start(self):
        self.each(lambda k: self.to_mate(self.turn(k)).start())

    def sum_mates(self, p):
        self.to_mate(p).wait_recv()
        here = self.rows(p)
        both = self.buf[self.rows(p, self.side * self.high)].astype(F32) + self.first[here].astype(F32)
        self.first[here] = both.astype(BF16)

        @pl.when(p != self.place)
        def _():
            self.to_owner(p, self.place).start()

    def sum_quarter(self, q):
        self.each(
            lambda k: self.sum_mates(self.turn(k)), q * self.count // 4, (q + 1) * self.count // 4
        )

    def sum_owners(self):
        self.second[self.rows(self.place)] = self.first[self.rows(self.place)]
        self.others(lambda q: self.to_owner(q, q).wait_recv())
        total = lax.fori_loop(
            0,
            self.count,
            lambda q, acc: acc + self.second[self.rows(q)].astype(F32),
            jnp.zeros((self.piece, self.buf.shape[1]), F32),
        )
        self.buf[self.rows(self.place, self.side * self.high)] = total.astype(BF16)
        self.others(lambda p: self.to_peer(p, self.place).start())
        self.back(self.place).start()

    def forward(self):
        def body(q):
            self.to_peer(q, q).wait_recv()
            self.back(q).start()

        self.others(body)

    def finish(self):
        self.each(lambda p: self.back(p).wait_recv())

    def take(self, body):
        for side in range(2):

            @pl.when(self.side == side)
            def _(side=side):
                body(side, self.buf.at[side * self.high : (side + 1) * self.high])
                body(1 - side, self.other)

    def drain(self):
        self.each(lambda p: self.to_mate(p).wait_send())
        self.others(lambda p: self.to_owner(p, self.place).wait_send())
        self.others(lambda p: self.to_peer(p, self.place).wait_send())
        self.each(lambda p: self.back(p).wait_send())


def scratch(count, width, hidden, groups):
    parts = D // width
    blocks = count // SHORT
    bf, f = BF16, F32
    arrays = dict(
        RES=((D, count), bf),
        COT=((D, count), bf),
        MIX=((D, count), bf),
        VEC=((parts, SUBLANES, 2 * LANES), f),
        COLS=((D, LANES), f),
        WO=((D, D), bf),
        WE=((D, hidden), bf),
        WET=((hidden, D), bf),
        WR=((hidden, D), bf),
        WN=((D, 3 * width), bf),
        QT=((width, count), bf),
        KT=((width, count), bf),
        VT=((width, count), bf),
        KN=((count, width), bf),
        VN=((count, width), bf),
        LSE=((blocks, SUBLANES, SHORT), f),
        TOK=((blocks, SUBLANES, SHORT), f),
        X1=((D, count), f),
        E2P=((D, count), bf),
        E2C=((blocks, D // 2, SHORT), bf),
        E2Y=((blocks, D // 2, SHORT), bf),
        E2T=((blocks, D // 2, SHORT), bf),
        PIECES=((2, parts, width, SHORT), bf),
        B2C=((2, blocks, width, SHORT), bf),
        B2Y=((blocks, width, SHORT), bf),
        E1C=((2, blocks, width, SHORT), bf),
        E1Y=((blocks, width, SHORT), bf),
        STAT=((parts, blocks, SUBLANES, SHORT), f),
        GWE=((D, hidden), f),
        GWR=((hidden, D), f),
        GW=((3 * width + width, D), f),
        ACC=((D, LANES), f),
        OWN=((3 * width, LANES), f),
        SQ=((parts, SUBLANES, SHORT), f),
        BM=((2 * D, hidden), bf),
        BM1=((D, hidden), bf),
        BM2=((D, hidden), bf),
        BT=((2 * D, 2 * width), bf),
        SMALL=((groups, 16, 2 * LANES), f),
    )
    sems = dict(
        load=(1, 8), store=(1, 8), bm=(4, groups // 2), bt=(4, groups // 2), tiny=(1, groups),
        res=(3, blocks), cot=(3, blocks), mix=(3, blocks), wo_=(3, 1), vec_=(3, 1), sq=(3, 1),
        e2a=(1, blocks), e2x=(1, blocks), e2b=(1, blocks),
        b2c=(2, blocks), b2x=(1, blocks), e1c=(2, blocks), e1x=(1, blocks), stat=(3, blocks),
    )
    names, shapes = [], []
    for name, (shape, dtype) in arrays.items():
        names.append(name)
        shapes.append(pltpu.VMEM(shape, dtype))
    for name, shape in sems.items():
        for way in ("s", "r"):
            names.append(f"{name}_{way}")
            shapes.append(pltpu.SemaphoreType.DMA(shape))
    return names, shapes


def layer_kernel(groups, names, *refs):
    n = types.SimpleNamespace(**dict(zip((*INPUTS, *OUTPUTS, *names), refs, strict=True)))
    width, count = n.res.shape
    parts = D // width
    blocks = count // SHORT
    heads = width // HEAD
    hidden = n.we.shape[1]
    me = lax.axis_index("mp")
    core = me + 1 - 2 * lax.rem(me, 2)
    across = lax.rem(me + parts // 2, parts)
    corner = lax.rem(core + parts // 2, parts)
    side = lax.rem(me, 2)
    peers = (core, across, corner)
    dp = lax.axis_index("dp")
    own = at(me, width)

    def tokens(i):
        return at(i, SHORT)

    loads = [
        pltpu.make_async_copy(src, dst, n.load_s.at[0, k])
        for k, (src, dst) in enumerate(
            (
                (n.w, n.BM.at[: 3 * width]),
                (n.wo, n.WO.at[own]),
                (n.res, n.RES.at[own]),
                (n.we, n.WE),
                (n.wr, n.WR),
                (n.cot, n.COT.at[own]),
            )
        )
    ]
    barrier = pltpu.get_barrier_semaphore()
    for peer in peers:
        pl.semaphore_signal(barrier, inc=1, device_id={"mp": peer}, device_id_type=MESH)

    def each_group(body):
        def run(d, _):
            body(d, lax.rem(dp + d, groups))
            return 0

        lax.fori_loop(1, groups, run, 0)

    each_group(
        lambda d, group: pl.semaphore_signal(
            barrier, inc=1, device_id={"dp": group}, device_id_type=MESH
        )
    )
    for c in loads:
        c.start()
    pl.semaphore_wait(barrier, len(peers) + groups - 1)

    feed = Reduce(n.BM, n.BM1, n.BM2, n.WET, (n.bm_s, n.bm_r), dp, groups)
    spare = (n.WE.at[:, : 2 * width], n.WE.at[:, 2 * width :], n.WR.at[:, : 2 * width])
    rest = Reduce(n.BT, *spare, (n.bt_s, n.bt_r), dp, groups)

    def gather(buf, source, sems):
        return Gather(
            lambda slot, i: buf.at[at(slot, width), tokens(i)],
            lambda i: source.at[:, tokens(i)],
            sems, me, core, across,
        )

    res = gather(n.RES, n.res, (n.res_s, n.res_r))
    cot = gather(n.COT, n.cot, (n.cot_s, n.cot_r))
    mix = gather(n.MIX, n.MIX.at[own], (n.mix_s, n.mix_r))
    weight = Gather(
        lambda slot, i: n.WO.at[at(slot, width)],
        lambda i: n.wo,
        (n.wo__s, n.wo__r), me, core, across,
    )

    def vec_copy(k):
        return copy_to(n.vec.at[:SUBLANES], n.VEC.at[me], n.vec__s.at[k, 0], n.vec__r.at[k, 0], peers[k])

    res.start(0)
    for k in range(3):
        vec_copy(k).start()
    for i in range(1, blocks):
        res.start(i)
    n.VEC[me] = n.vec[:SUBLANES]
    loads[0].wait()
    n.WN[...] = jnp.transpose(n.BM[: 3 * width])
    for ref in (n.GWE, n.GWR, n.GW, n.ACC, n.OWN, n.SQ):
        ref[...] = jnp.zeros_like(ref)
    total = n.lengths[0, 0]
    for slot in range(1, n.lengths.shape[1]):
        total = total + n.lengths[0, slot]
    far = jnp.where(n.lengths[0, 0] == LONG, 0.0, FAR)
    for c in loads[1:5]:
        c.wait()
    n.WET[...] = jnp.transpose(n.WE[...])
    for k in range(2):
        n.BT[k * D : (k + 1) * D] = jnp.transpose(n.WR[k * 2 * width : (k + 1) * 2 * width])
    for k in range(3):
        vec_copy(k).wait_recv()
    vectors = jnp.concatenate([n.VEC[p][:, :width] for p in range(parts)], axis=1)
    be = jnp.concatenate(
        [n.vec[SUBLANES + p : SUBLANES + p + 1, :width] for p in range(parts)], axis=1
    )
    vectors = jnp.where(rows_of(vectors.shape) == 6, be, vectors)
    vectors = jnp.concatenate([vectors, jnp.zeros((LANES - SUBLANES, D), F32)], axis=0)
    n.COLS[...] = jnp.transpose(vectors)
    loads[5].wait()

    def col(k):
        return n.COLS[:, k : k + 1]

    def own_col(k):
        return n.COLS[own, k : k + 1]

    def halves(values):
        pair = values[: 2 * HEAD]
        row = rows_of(pair.shape)
        zero = jnp.zeros_like(pair)
        return (jnp.where(row < HEAD, pair, zero), jnp.where(row < HEAD, zero, pair), values[2 * HEAD :])

    def part_of(values, h):
        return values[:, : 2 * HEAD] if h < 2 else values[:, 2 * HEAD :]

    def head_rows(values, h):
        return values[h * HEAD : (h + 1) * HEAD]

    def forward_block(i, _):
        res.forward(i)

        @pl.when(i == 2)
        def _():
            weight.start(0)
            cot.start(0)

        res.finish(i)
        here = tokens(i)
        full, inverse = decompress(n.RES[:, here].astype(F32))
        rows = (full * inverse * col(0)).astype(BF16)
        qkv = dot(n.BM[: 3 * width], rows)
        q = (qkv[:width] + own_col(4)).astype(BF16)
        k = qkv[width : 2 * width].astype(BF16)
        v = (qkv[2 * width :] + own_col(5)).astype(BF16)
        k_rows = jnp.transpose(k)
        n.QT[:, here] = q
        n.KT[:, here] = k
        n.VT[:, here] = v
        n.KN[here] = k_rows
        n.VN[here] = jnp.transpose(v)
        live = i * SHORT < total
        allowed = diagonal(live)
        q_heads = halves(q * SCORE_SCALE)
        carry = []
        for h in range(heads):
            s = jnp.where(allowed, dot(part_of(k_rows, h), q_heads[h]), -FAR)
            m = jnp.max(s, axis=0, keepdims=True)
            p = jnp.exp(s - m)
            carry.append((m, column_sum(p), dot(head_rows(v, h), p.astype(BF16))))

        def body(j, carry):
            k_j = n.KN[tokens(j)]
            v_j = n.VT[:, tokens(j)]
            after = []
            for h in range(heads):
                m, norm, acc = carry[h]
                s = dot(part_of(k_j, h), q_heads[h])
                new = jnp.maximum(m, jnp.max(s, axis=0, keepdims=True) - far)
                p = jnp.exp(s - (new + far))
                scale = jnp.exp(m - new)
                after.append(
                    (new, norm * scale + column_sum(p), acc * scale + dot(head_rows(v_j, h), p.astype(BF16)))
                )
            return after

        carry = lax.fori_loop(0, i, body, carry)
        mixed = []
        for h in range(heads):
            m, norm, acc = carry[h]
            mixed.append(acc / norm)
            n.LSE[i, h : h + 1] = m + jnp.log(norm)
        n.MIX[own, here] = jnp.concatenate(mixed, axis=0).astype(BF16)

        @pl.when(i == 0)
        def _():
            mix.start(i)

        return 0

    lax.fori_loop(0, blocks, forward_block, 0)

    high = D // 2

    def e2_half(i, which):
        return n.E2P.at[at(which, high), tokens(i)]

    def e2_first(i):
        return copy_to(e2_half(i, 1 - side), n.E2C.at[i], n.e2a_s.at[0, i], n.e2a_r.at[0, i], core)

    def e2_cross(i):
        return copy_to(n.E2C.at[i], n.E2Y.at[i], n.e2x_s.at[0, i], n.e2x_r.at[0, i], across)

    def e2_last(i):
        return copy_to(e2_half(i, side), n.E2T.at[i], n.e2b_s.at[0, i], n.e2b_r.at[0, i], core)

    def e2_sum(i):
        e2_first(i).wait_recv()
        mine = n.E2P[at(side, high), tokens(i)].astype(F32)
        n.E2C[i] = (mine + n.E2C[i].astype(F32)).astype(BF16)
        e2_cross(i).start()

    def e2_total(i):
        e2_cross(i).wait_recv()
        both = n.E2C[i].astype(F32) + n.E2Y[i].astype(F32)
        n.E2P[at(side, high), tokens(i)] = both.astype(BF16)
        e2_last(i).start()

    def scatter_first(C, sems, slot, i):
        targets = (core, corner)
        return [
            copy_to(
                n.PIECES.at[slot, targets[k]], C.at[k, i], sems[0].at[k, i], sems[1].at[k, i], core
            )
            for k in range(2)
        ]

    def scatter_sum(C, first, slot, i):
        for c in first:
            c.wait_recv()
        for k, owner in enumerate((me, across)):
            C[k, i] = (n.PIECES[slot, owner].astype(F32) + C[k, i].astype(F32)).astype(BF16)

    def scatter_cross(C, Y, sems, i):
        return copy_to(C.at[1, i], Y.at[i], sems[0].at[0, i], sems[1].at[0, i], across)

    def b2_first(slot, i):
        return scatter_first(n.B2C, (n.b2c_s, n.b2c_r), slot, i)

    def b2_cross(i):
        return scatter_cross(n.B2C, n.B2Y, (n.b2x_s, n.b2x_r), i)

    def e1_first(slot, i):
        return scatter_first(n.E1C, (n.e1c_s, n.e1c_r), slot, i)

    def e1_cross(i):
        return scatter_cross(n.E1C, n.E1Y, (n.e1x_s, n.e1x_r), i)

    def split(slot, values):
        for p in range(parts):
            n.PIECES[slot, p] = values[p * width : (p + 1) * width]

    def order(step):
        return lax.rem(blocks - step, blocks)

    for i in range(blocks - 1, 0, -1):
        mix.start(i)
        cot.start(i)
    mix.forward(0)
    weight.forward(0)
    cot.forward(0)
    weight.finish(0)
    n.BM[D:] = jnp.transpose(n.WO[...])

    def middle_block(step, _):
        i = order(step)
        slot = lax.rem(step, 2)

        @pl.when(step >= 1)
        def _():
            mix.forward(i)
            cot.forward(i)

        mix.finish(i)
        cot.finish(i)
        here = tokens(i)
        full, _unused = decompress(n.RES[:, here].astype(F32))
        x1 = full + center(dot(n.BM[D:], n.MIX[:, here]) + col(1))
        n.X1[:, here] = x1
        rows = (x1 * inverse_rms(x1) * col(2)).astype(BF16)
        z = dot(n.WET[...], rows) + col(6)
        square = z * z
        h = 0.5 + 0.5 * jnp.tanh(z * (0.7978845608 + (0.7978845608 * 0.044715) * square))
        active = z * h
        slope = h + active * (1.0 - h) * (
            2 * 0.7978845608 + (6 * 0.7978845608 * 0.044715) * square
        )
        active = active.astype(BF16)
        slope = slope.astype(BF16)

        @pl.when(step >= 2)
        def _():
            e2_sum(order(step - 1))
            for c in b2_first(slot, order(step - 2)):
                c.wait_send()

        @pl.when(step >= 1)
        def _():
            before = order(step - 1)
            scatter_sum(n.B2C, b2_first(1 - slot, before), 1 - slot, before)

        b2 = dot(n.BT[:D], active[: 2 * width]) + dot(n.BT[D:], active[2 * width :])
        split(slot, center(b2).astype(BF16))
        for c in b2_first(slot, i):
            c.start()
        g2 = branch_grad(n.COT[:, here].astype(F32)).astype(BF16)
        n.GWR[...] += dot_nt(active, g2)
        d_hidden = (dot(n.WR[...], g2) * slope).astype(BF16)
        n.ACC[...] += dot(g2, pick(0)) + dot(d_hidden, pick(1))
        n.GWE[...] += dot_nt(rows, d_hidden)
        n.E2P[:, here] = dot(n.WE[...], d_hidden).astype(BF16)
        e2_first(i).start()
        return 0

    lax.fori_loop(0, blocks, middle_block, 0)
    last = (blocks - 1) % 2
    e2_sum(order(blocks - 1))
    e2_sum(0)
    scatter_sum(n.B2C, b2_first(last, order(blocks - 1)), last, order(blocks - 1))
    n.BM[:D] = n.GWE[...].astype(BF16)
    n.BM[D:] = n.GWR[...].astype(BF16)
    feed.start()
    for slot, step in ((1 - last, blocks - 2), (last, blocks - 1)):
        for c in b2_first(slot, order(step)):
            c.wait_send()
    n.GWE[...] = jnp.zeros_like(n.GWE)
    n.GWR[...] = jnp.zeros_like(n.GWR)

    def stat_copy(k, i):
        mine = n.STAT.at[me, i]
        return copy_to(mine, mine, n.stat_s.at[k, i], n.stat_r.at[k, i], peers[k])

    stored = rows_of((width, 1)) + me * width < D - 1

    def finish_grad(i):
        here = tokens(i)
        e1_cross(i).wait_recv()
        for k in range(3):
            stat_copy(k, i).wait_recv()
        stat = n.STAT[0, i]
        for p in range(1, parts):
            stat = stat + n.STAT[p, i]
        along, c_last = stat[0:1], stat[1:2]
        inverse, u_last, g_last = n.TOK[i, 0:1], n.TOK[i, 1:2], n.TOK[i, 2:3]
        e1 = n.E1C[0, i].astype(F32) + n.E1Y[i].astype(F32)
        u_own = jnp.where(stored, n.RES[own, here].astype(F32), u_last)
        normed = e1 * u_own * inverse
        n.OWN[:width] += dot(normed.astype(BF16), pick(3))
        cube = inverse * inverse * inverse * along / D
        result = n.X1[at(across, width), here] + inverse * (e1 * own_col(0)) - u_own * cube
        final = g_last + inverse * c_last - u_last * cube
        n.QT[:, here] = jnp.where(stored, result - final, 0.0).astype(BF16)

    def finish_out(i):
        here = tokens(i)
        b2_cross(i).wait_recv()
        b2 = n.B2C[0, i].astype(F32) + n.B2Y[i].astype(F32)
        x2 = n.X1[own, here] + b2 + (own_col(3) - jnp.mean(col(3), axis=0, keepdims=True))
        n.VT[:, here] = jnp.where(stored, x2, 0.0).astype(BF16)
        live = lanes((1, SHORT)) + i * SHORT < total
        n.SQ[me, 0:1] += jnp.where(live, column_sum(x2 * x2), 0.0)

    def backward_block(step, _):
        i = blocks - 1 - step
        slot = lax.rem(step, 2)
        here = tokens(i)

        @pl.when(step == 0)
        def _():
            e2_total(i)

        @pl.when(step == 1)
        def _():
            for b in range(blocks):
                b2_cross(b).start()

        e2_last(i).wait_recv()
        e2_first(i).wait_send()
        n.E2P[at(1 - side, high), here] = n.E2T[i]
        x1 = n.X1[:, here]
        inverse = inverse_rms(x1)
        e2 = n.E2P[:, here].astype(F32)
        normed = e2 * x1
        gain_part = (normed * inverse).astype(BF16)
        along = column_sum(normed * col(2))
        du = inverse * (e2 * col(2)) - x1 * (inverse * inverse * inverse * along / D)
        g1 = branch_grad(n.COT[:, here].astype(F32)) + center(du)
        n.TOK[i, 2:3] = g1[D - 1 :]
        for p in range(parts):

            @pl.when(me == p)
            def _():
                n.X1[at(across, width), here] = g1[p * width : (p + 1) * width]

        g1 = g1.astype(BF16)
        n.ACC[...] += dot(gain_part, pick(2)) + dot(g1, pick(3))
        mixed = n.MIX[own, here]
        n.GW[3 * width :] += dot_nt(mixed, g1)
        d_mixed = dot(n.WO[own], g1).astype(BF16)
        product = d_mixed.astype(F32) * mixed.astype(F32)
        delta = [column_sum(head_rows(product, h)) for h in range(heads)]
        lse = [n.LSE[i, h : h + 1] for h in range(heads)]
        live = i * SHORT < total
        q = n.QT[:, here] * SCORE_SCALE
        q_heads = halves(q)
        g_heads = halves(d_mixed)

        def pair(j, lse, allowed):
            there = tokens(j)
            k_j, v_j, k_t = n.KN[there], n.VN[there], n.KT[:, there]
            dq, dk, dv = [], [], []
            for h in range(heads):
                p = jnp.exp(dot(part_of(k_j, h), q_heads[h]) - lse[h])
                if allowed is not None:
                    p = jnp.where(allowed, p, 0.0)
                dv.append(dot_nt(head_rows(d_mixed, h), p.astype(BF16)))
                p = (p * (dot(part_of(v_j, h), g_heads[h]) - delta[h])).astype(BF16)
                dk.append(dot_nt(head_rows(q, h), p))
                dq.append(dot(head_rows(k_t, h), p))
            n.GWE[at(j, width), :SHORT] += jnp.concatenate(dv, axis=0)
            n.GWR[at(j, width), :SHORT] += jnp.concatenate(dk, axis=0)
            return jnp.concatenate(dq, axis=0)

        dq = pair(i, lse, diagonal(live))

        @pl.when(i >= 1)
        def _():
            e2_total(i - 1)

        @pl.when(step == 1)
        def _():
            feed.sum_quarter(2)

        @pl.when(step == blocks - 1)
        def _():
            feed.sum_owners()

        @pl.when(step >= 1)
        def _():
            scatter_sum(n.E1C, e1_first(1 - slot, i + 1), 1 - slot, i + 1)
            e1_cross(i + 1).start()

        lse_far = [row + far for row in lse]

        def body(j, dq):
            dq = dq + pair(j, lse_far, None)

            @pl.when((step == 0) & (j != 1))
            def _():
                feed.sum_quarter(lax.div(j, 2))

            @pl.when((step == 1) & (j == 0))
            def _():
                feed.sum_quarter(3)

            return dq

        dq = lax.fori_loop(0, i, body, dq)
        d_all = jnp.concatenate(
            [dq * SCORE_SCALE, n.GWR[at(i, width), :SHORT], n.GWE[at(i, width), :SHORT]], axis=0
        ).astype(BF16)
        n.OWN[...] += dot(d_all, pick(0))
        full, inverse = decompress(n.RES[:, here].astype(F32))
        rows = (full * inverse * col(0)).astype(BF16)
        n.GW[: 3 * width] += dot_nt(d_all, rows)
        e1 = dot(n.WN[...], d_all)

        @pl.when(step >= 2)
        def _():
            for c in e1_first(slot, i + 2):
                c.wait_send()

        split(slot, e1.astype(BF16))
        for c in e1_first(slot, i):
            c.start()
        c = e1 * col(0)
        n.STAT[me, i, 0:1] = column_sum(c * full)
        n.STAT[me, i, 1:2] = c[D - 1 :]
        for k in range(3):
            stat_copy(k, i).start()
        n.TOK[i, 0:1] = inverse
        n.TOK[i, 1:2] = full[D - 1 :]
        return 0

    lax.fori_loop(0, blocks, backward_block, 0)
    scatter_sum(n.E1C, e1_first(last, 0), last, 0)
    e1_cross(0).start()
    n.BT[:D] = n.GW[:, : 2 * width].astype(BF16)
    n.BT[D:] = n.GW[:, 2 * width :].astype(BF16)
    rest.start()

    def square_copy(k):
        return copy_to(n.SQ.at[me], n.SQ.at[me], n.sq_s.at[k, 0], n.sq_r.at[k, 0], peers[k])

    def finish_block(k, _):
        finish_out(k)
        rest.sum_quarter(k)
        return 0

    lax.fori_loop(0, blocks, finish_block, 0)
    for k in range(3):
        square_copy(k).start()

    def finish_rows(k, _):
        finish_grad(blocks - 1 - k)
        return 0

    feed.forward()
    lax.fori_loop(0, blocks, finish_rows, 0)
    for k in range(3):
        square_copy(k).wait_recv()

    def tiny_copy(slot, group):
        here = n.SMALL.at[dp]
        return pltpu.make_async_remote_copy(
            src_ref=here,
            dst_ref=here,
            send_sem=n.tiny_s.at[0, group],
            recv_sem=n.tiny_r.at[0, slot],
            device_id={"dp": group},
            device_id_type=MESH,
        )

    squares = jnp.sum(sum(n.SQ[p, 0:1] for p in range(parts)), axis=1, keepdims=True)
    mine = n.ACC[own]
    parts_in = [
        n.OWN[:width, 0:1],
        n.OWN[2 * width :, 0:1],
        n.OWN[:width, 3:4],
        squares,
        mine[:, 3:4],
        mine[:, 2:3],
        mine[:, 0:1],
        total.astype(F32),
    ] + [n.ACC[p * width : (p + 1) * width, 1:2] for p in range(parts)]
    table = jnp.zeros((width, LANES), F32)
    for lane, values in enumerate(parts_in):
        table = jnp.where(lanes(table.shape) == lane, values, table)
    table = jnp.concatenate([table, jnp.zeros((2 * LANES - width, LANES), F32)], axis=0)
    n.SMALL[dp] = jnp.transpose(table)[:16]
    each_group(lambda d, group: tiny_copy(dp, group).start())

    def store(src, dst, k):
        return pltpu.make_async_copy(src, dst, n.store_s.at[0, k])

    stores = [store(n.QT, n.grad, 0), store(n.VT, n.out, 1)]
    for c in stores:
        c.start()
    rest.sum_owners()
    each_group(lambda d, group: tiny_copy(group, group).wait_recv())
    small = n.SMALL[0]
    for group in range(1, groups):
        small = small + n.SMALL[group]
    n.small[...] = small
    feed.finish()

    def store_half(target, k):
        def body(half, rows):
            store(rows, target.at[half * D : (half + 1) * D], k + half).start()

        return body

    feed.take(store_half(n.feed, 2))
    rest.forward()
    rest.finish()
    rest.take(store_half(n.rest, 4))
    for k, (buf, target) in enumerate(((n.BM, n.feed), (n.BT, n.rest))):
        for half in range(2):
            here = slice(half * D, (half + 1) * D)
            stores.append(store(buf.at[here], target.at[here], 2 + 2 * k + half))

    for k in range(3):
        vec_copy(k).wait_send()
        square_copy(k).wait_send()
    weight.drain(0)

    def drain(i, _):
        for g in (res, cot, mix):
            g.drain(i)
        for c in (e2_cross, e2_last, b2_cross, e1_cross):
            c(i).wait_send()
        for k in range(3):
            stat_copy(k, i).wait_send()
        return 0

    lax.fori_loop(0, blocks, drain, 0)
    for step in (blocks - 2, blocks - 1):
        for c in e1_first(step % 2, blocks - 1 - step):
            c.wait_send()
    for c in stores:
        c.wait()
    feed.drain()
    rest.drain()
    each_group(lambda d, group: tiny_copy(dp, group).wait_send())


def finish_kernel(
    out, grad, rest_low, rest_high, feed_low, feed_high, small,
    out_ref, grad_ref, gw_ref, gwo_ref, gwe_ref, gwr_ref,
    gb_ref, gbo_ref, gg_one_ref, gg_two_ref, gbe_ref, gbr_ref, rms_ref, live_ref,
):
    i = pl.program_id(0)
    width = gb_ref.shape[1]
    out_ref[...] = out[...]
    grad_ref[...] = grad[...]
    rest = jnp.concatenate([rest_low[...], rest_high[...]], axis=1).astype(F32)
    gwe_ref[...] = feed_low[...].astype(F32)
    gwr_ref[...] = feed_high[...].astype(F32)

    @pl.when(i < 3)
    def _():
        gw_ref[...] = rest

    @pl.when(i == 3)
    def _():
        gwo_ref[...] = rest

    @pl.when(i == 0)
    def _():
        gb_ref[...] = small[0:2, :width]
        gg_one_ref[...] = small[2:3, :width]
        gbo_ref[...] = small[4:5, :width]
        gg_two_ref[...] = small[5:6, :width]
        gbr_ref[...] = small[6:7, :width]
        gbe_ref[...] = jnp.concatenate(
            [small[8 + p : 9 + p, :width] for p in range(D // width)], axis=1
        )
        live = small[7:8, 0:1]
        rms_ref[...] = jnp.sqrt(small[3:4, 0:1] / (D * live))
        live_ref[...] = live.astype(jnp.int32)


def on_device(
    residual,
    lengths,
    gain_one,
    input_weight,
    input_bias,
    output_weight,
    output_bias,
    gain_two,
    expand_weight,
    expand_bias,
    reduce_weight,
    reduce_bias,
    cotangent,
):
    count, width = residual.shape
    hidden = expand_weight.shape[1]
    parts = D // width

    def shape(*dims, dtype=F32):
        return jax.ShapeDtypeStruct(dims, dtype)

    zero = jnp.zeros((2, width), F32)
    vec = jnp.concatenate(
        [gain_one[None], output_bias[None], gain_two[None], reduce_bias[None], input_bias, zero]
        + [expand_bias.reshape(parts, width), zero, zero]
    )
    vec = jnp.pad(vec, ((0, 0), (0, 2 * LANES - width)))
    groups = lax.axis_size("dp")
    names, scratches = scratch(count, width, hidden, groups)

    def space(name):
        return pl.BlockSpec(memory_space=pltpu.VMEM if name in IN_VMEM else pl.ANY)

    out, grad, rest, feed, small = pl.pallas_call(
        lambda *refs: layer_kernel(groups, names, *refs),
        in_specs=[pl.BlockSpec(memory_space=pltpu.SMEM)] + [space(name) for name in INPUTS[1:]],
        out_specs=[space(name) for name in OUTPUTS],
        out_shape=[
            shape(width, count, dtype=BF16),
            shape(width, count, dtype=BF16),
            shape(2 * D, 2 * width, dtype=BF16),
            shape(2 * D, hidden, dtype=BF16),
            shape(16, 2 * LANES),
        ],
        scratch_shapes=scratches,
        compiler_params=pltpu.CompilerParams(
            vmem_limit_bytes=63 << 20, collective_id=0, has_side_effects=True
        ),
        name="layer",
    )(
        lengths,
        residual.T,
        cotangent.T,
        vec,
        jnp.transpose(input_weight, (0, 2, 1)).reshape(3 * width, D),
        output_weight,
        expand_weight,
        reduce_weight,
    )

    def rows(high, wide, base=0):
        return pl.BlockSpec((high, wide), lambda i: (i + base, 0))

    def whole(*dims):
        return pl.BlockSpec(dims, lambda i: (0,) * len(dims))

    def clip(high, wide, first, last):
        return pl.BlockSpec((high, wide), lambda i: (jnp.clip(i - first, 0, last - first), 0))

    step = D // parts
    thin = width // parts
    out, grad, gw, gwo, gwe, gwr, *vectors = pl.pallas_call(
        finish_kernel,
        grid=(parts,),
        in_specs=[
            rows(thin, count),
            rows(thin, count),
            rows(step, 2 * width),
            rows(step, 2 * width, parts),
            rows(step, hidden),
            rows(step, hidden, parts),
            whole(16, 2 * LANES),
        ],
        out_specs=[
            rows(thin, count),
            rows(thin, count),
            clip(width, D, 0, 2),
            clip(width, D, 3, 3),
            rows(step, hidden),
            rows(step, hidden),
            whole(2, width),
            whole(1, width),
            whole(1, width),
            whole(1, width),
            whole(1, hidden),
            whole(1, width),
            whole(1, 1),
            whole(1, 1),
        ],
        out_shape=[
            shape(width, count, dtype=BF16),
            shape(width, count, dtype=BF16),
            shape(3 * width, D),
            shape(width, D),
            shape(D, hidden),
            shape(hidden, D),
            shape(2, width),
            shape(1, width),
            shape(1, width),
            shape(1, width),
            shape(1, hidden),
            shape(1, width),
            shape(1, 1),
            shape(1, 1, dtype=jnp.int32),
        ],
        compiler_params=pltpu.CompilerParams(vmem_limit_bytes=60 << 20),
        name="finish",
    )(out, grad, rest, rest, feed, feed, small)
    gb, gbo, gg_one, gg_two, gbe, gbr, rms, live_count = vectors
    return (
        out.T,
        grad.T,
        jnp.transpose(gw.reshape(3, width, D), (0, 2, 1)),
        gb,
        gwo,
        gbo[0],
        gg_one[0],
        gg_two[0],
        gwe,
        gbe[0],
        gwr,
        gbr[0],
        rms[0, 0],
        live_count[0, 0],
    )


def solution(mesh):
    return jax.shard_map(
        on_device,
        mesh=mesh,
        in_specs=(
            P("dp", "mp"),
            P("dp", None),
            P("mp"),
            P(None, None, "mp"),
            P(None, "mp"),
            P("mp", None),
            P("mp"),
            P("mp"),
            P(None, "mp"),
            P("mp"),
            P("mp", None),
            P("mp"),
            P("dp", "mp"),
        ),
        out_specs=(
            P("dp", "mp"),
            P("dp", "mp"),
            P(None, None, "mp"),
            P(None, "mp"),
            P("mp", None),
            P("mp"),
            P("mp"),
            P("mp"),
            P(None, "mp"),
            P("mp"),
            P("mp", None),
            P("mp"),
            P(),
            P(),
        ),
        check_vma=False,
    )
```

time: 241 us -> 201 us (0.83); the launches traced: 237 us -> 200 us
  local copies, waits for them, and re-layouts: 22.9 us -> 2.17 us
  Pallas kernels: 208 us -> 196 us
  between operations: 4.94 us -> 0.66 us
    pallas_call x1, Pallas kernels: 208 us -> 189 us  [on_device(): pl.pallas_call(lambda *refs: layer_kernel(groups, names, *refs), in_specs...]
    unnamed x21 -> x0, local copies, waits for them, and re-layouts: 16.2 us -> none
    pallas_call x0 -> x1, Pallas kernels: none -> 6.65 us  [on_device(): pl.pallas_call(finish_kernel, grid=(parts,), in_specs=[rows(thin, count),...]
    slice x4 -> x0, local copies, waits for them, and re-layouts: 4.67 us -> none  [the longest x1 1.42 us: on_device(): small[6]]
where the time goes in v3:
time: 201 us; the launch traced here: 200 us
  Pallas kernels  196 us (98%)
  local copies, waits for them, and re-layouts  2.17 us (1%)
    pallas_call x1, Pallas kernels, on_device(): pl.pallas_call(lambda *refs: layer_kernel(groups, names, *refs), in_specs...  189 us
    pallas_call x1, Pallas kernels, on_device(): pl.pallas_call(finish_kernel, grid=(parts,), in_specs=[rows(thin, count),...  6.65 us

profile of v3, /device:TPU:0, one launch (start us, length us, event | category | flops | bytes accessed | tf_op | source)
XLA Modules:
  0.0 199.7 jit_solution(14584886603531530555)
XLA Ops:
  0.6 0.8 reshape.37
  1.4 0.8 concatenate.7
  2.2 0.6 pad.4.refs_3_
  2.8 189.0 %layer.1 = (bf16[192,2048]{1,0:T(8,128)(2,1)}, bf16[192,2048]{1,0:T(8,128)(2,1)}, bf16[1536,384]{1,0:T(8,128)(2,1)}, bf16[1536,768]{1,0:T(8,128)(2,1)}, f32[16,256]{1,0:T(8,128)}) custom-call(s32[1,4]{1,0:T(1,128)} %refs_0_.1, bf16[192,2048]{1,0:T(8,128)(2,1)} %bitcast.21, bf16[192,2048]{1,0:T(8,128)(2,1)} %bitcast.22, f32[16,256]{1,0:T(8,128)} %pad.4.refs_3_, ...), custom_call_target="tpu_custom_call" | custom-call | tf_op jit(solution)/shard_map/layer/pallas_call | solution.py:971
  191.8 6.7 %finish.1 = (bf16[192,2048]{1,0:T(8,128)(2,1)}, bf16[192,2048]{1,0:T(8,128)(2,1)}, f32[576,768]{1,0:T(8,128)}, f32[192,768]{1,0:T(8,128)}, f32[768,768]{1,0:T(8,...) custom-call(bf16[192,2048]{1,0:T(8,128)(2,1)} %get-tuple-element.33., ...), custom_call_target="tpu_custom_call" | custom-call | tf_op jit(solution)/shard_map/finish/pallas_call | solution.py:1009
  198.4 1.3 reduce
  (2 shorter events, 0.0 us)

commit v4 on v3

--- a/solution.py
+++ b/solution.py
@@ -124,9 +124,67 @@
             self.copy(kind, i).wait_send()
 
 
-INPUTS = ("lengths", "res", "cot", "vec", "w", "wo", "we", "wr")
+class WeightGather:
+    def __init__(self, buf, source, sems, places):
+        self.buf, self.source, self.sems = buf, source, sems
+        self.me, self.core, self.across, self.side, self.mate = places
+        self.width = source.shape[0]
+
+    def rows(self, slot, half=None):
+        size = self.width if half is None else self.width // 2
+        base = slot * self.width + (0 if half is None else half * size)
+        return self.buf.at[pl.ds(pl.multiple_of(base, size), size)]
+
+    def copy(self, src, dst, kind, peer):
+        return pltpu.make_async_remote_copy(
+            src_ref=src,
+            dst_ref=dst,
+            send_sem=self.sems[0].at[kind, 0],
+            recv_sem=self.sems[1].at[kind, 0],
+            device_id=peer,
+            device_id_type=MESH,
+        )
+
+    def to_core(self):
+        return self.copy(self.source, self.rows(self.me), 0, {"mp": self.core})
+
+    def to_across(self):
+        half = self.width // 2
+        cut = self.source.at[pl.ds(pl.multiple_of(self.side * half, half), half)]
+        return self.copy(cut, self.rows(self.me, self.side), 1, {"mp": self.across})
+
+    def to_mate(self):
+        got = self.rows(self.across, self.side)
+        return self.copy(got, got, 2, {"dp": self.mate})
+
+    def onward(self):
+        block = self.rows(self.across)
+        return self.copy(block, block, 3, {"mp": self.core})
+
+    def start(self):
+        self.to_across().start()
+        self.to_core().start()
+
+    def relay(self):
+        self.to_across().wait_recv()
+        self.to_mate().start()
+
+    def forward(self):
+        self.to_mate().wait_recv()
+        self.onward().start()
+
+    def finish(self):
+        self.to_core().wait_recv()
+        self.onward().wait_recv()
+
+    def drain(self):
+        for c in (self.to_core(), self.to_across(), self.to_mate(), self.onward()):
+            c.wait_send()
+
+
+INPUTS = ("lengths", "res", "cot", "v1", "v2", "v3", "v4", "ib", "be", "w", "wo", "we", "wr")
 OUTPUTS = ("out", "grad", "rest", "feed", "small")
-IN_VMEM = ("vec", "small")
+IN_VMEM = ("v1", "v2", "v3", "v4", "ib", "be", "small")
 
 
 class Reduce:
@@ -146,12 +204,12 @@
     def own(self, p):
         return self.buf.at[self.rows(p, self.side * self.high)]
 
-    def copy(self, src, dst, stage, p, slot, peer):
+    def copy(self, src, dst, stage, p, slot, peer, arrive=None):
         return pltpu.make_async_remote_copy(
             src_ref=src,
             dst_ref=dst,
             send_sem=self.sems[0].at[stage, p],
-            recv_sem=self.sems[1].at[stage, slot],
+            recv_sem=self.sems[1].at[stage if arrive is None else arrive, slot],
             device_id={"dp": peer},
             device_id_type=MESH,
         )
@@ -165,8 +223,10 @@
             self.first.at[self.rows(p)], self.second.at[self.rows(slot)], 1, p, slot, 2 * p + self.side
         )
 
-    def to_peer(self, p, slot):
-        return self.copy(self.own(slot), self.own(slot), 2, p, slot, 2 * p + self.side)
+    def onward(self, q, way):
+        place = self.place + way
+        piece = self.own(q)
+        return self.copy(piece, piece, 2 if way > 0 else 4, q, q, 2 * place + self.side, 2)
 
     def back(self, p):
         return self.copy(self.own(p), self.other.at[self.rows(p)], 3, p, p, self.mate)
@@ -187,8 +247,8 @@
         self.each(run)
 
     def turn(self, k):
-        half = self.count // 2
-        return lax.rem(k, 2) * half + lax.div(k, 2)
+        near = lax.div(k, 2)
+        return jnp.where(lax.rem(k, 2) == 0, near, self.count - 1 - near)
 
     def start(self):
         self.each(lambda k: self.to_mate(self.turn(k)).start())
@@ -218,15 +278,30 @@
             jnp.zeros((self.piece, self.buf.shape[1]), F32),
         )
         self.buf[self.rows(self.place, self.side * self.high)] = total.astype(BF16)
-        self.others(lambda p: self.to_peer(p, self.place).start())
+        self.pass_on(self.place, True, True)
         self.back(self.place).start()
 
-    def forward(self):
-        def body(q):
-            self.to_peer(q, q).wait_recv()
-            self.back(q).start()
-
-        self.others(body)
+    def pass_on(self, q, up, down):
+        @pl.when(up & (self.place < self.count - 1))
+        def _():
+            self.onward(q, 1).start()
+
+        @pl.when(down & (self.place > 0))
+        def _():
+            self.onward(q, -1).start()
+
+    def forward(self, third):
+        def body(d):
+            for q, up in ((self.place - d, True), (self.place + d, False)):
+
+                @pl.when((q >= 0) & (q < self.count))
+                def _(q=q, up=up):
+                    self.onward(q, 1).wait_recv()
+                    self.pass_on(q, up, not up)
+                    self.back(q).start()
+
+        far = self.count - 1
+        self.each(body, 1 + third * far // 3, 1 + (third + 1) * far // 3)
 
     def finish(self):
         self.each(lambda p: self.back(p).wait_recv())
@@ -242,7 +317,16 @@
     def drain(self):
         self.each(lambda p: self.to_mate(p).wait_send())
         self.others(lambda p: self.to_owner(p, self.place).wait_send())
-        self.others(lambda p: self.to_peer(p, self.place).wait_send())
+        def sent(q):
+            @pl.when((q <= self.place) & (self.place < self.count - 1))
+            def _():
+                self.onward(q, 1).wait_send()
+
+            @pl.when((q >= self.place) & (self.place > 0))
+            def _():
+                self.onward(q, -1).wait_send()
+
+        self.each(sent)
         self.each(lambda p: self.back(p).wait_send())
 
 
@@ -254,6 +338,7 @@
         RES=((D, count), bf),
         COT=((D, count), bf),
         MIX=((D, count), bf),
+        VIN=((SUBLANES, 2 * LANES), f),
         VEC=((parts, SUBLANES, 2 * LANES), f),
         COLS=((D, LANES), f),
         WO=((D, D), bf),
@@ -292,8 +377,8 @@
         SMALL=((groups, 16, 2 * LANES), f),
     )
     sems = dict(
-        load=(1, 8), store=(1, 8), bm=(4, groups // 2), bt=(4, groups // 2), tiny=(1, groups),
-        res=(3, blocks), cot=(3, blocks), mix=(3, blocks), wo_=(3, 1), vec_=(3, 1), sq=(3, 1),
+        load=(1, 8), store=(1, 8), bma=(5, groups // 2), bmb=(5, groups // 2), bt=(5, groups // 2), tiny=(1, groups),
+        res=(3, blocks), cot=(3, blocks), mix=(3, blocks), wo_=(4, 1), vec_=(3, 1), sq=(3, 1),
         e2a=(1, blocks), e2x=(1, blocks), e2b=(1, blocks),
         b2c=(2, blocks), b2x=(1, blocks), e1c=(2, blocks), e1x=(1, blocks), stat=(3, blocks),
     )
@@ -360,7 +445,12 @@
         c.start()
     pl.semaphore_wait(barrier, len(peers) + groups - 1)
 
-    feed = Reduce(n.BM, n.BM1, n.BM2, n.WET, (n.bm_s, n.bm_r), dp, groups)
+    feeds = []
+    for batch, sems in enumerate(((n.bma_s, n.bma_r), (n.bmb_s, n.bmb_r))):
+        cut = slice(batch * 2 * width, (batch + 1) * 2 * width)
+        views = [buf.at[:, cut] for buf in (n.BM, n.BM1, n.BM2, n.WET)]
+        feeds.append(Reduce(*views, sems, dp, groups))
+    feed, feed_late = feeds
     spare = (n.WE.at[:, : 2 * width], n.WE.at[:, 2 * width :], n.WR.at[:, : 2 * width])
     rest = Reduce(n.BT, *spare, (n.bt_s, n.bt_r), dp, groups)
 
@@ -374,21 +464,24 @@
     res = gather(n.RES, n.res, (n.res_s, n.res_r))
     cot = gather(n.COT, n.cot, (n.cot_s, n.cot_r))
     mix = gather(n.MIX, n.MIX.at[own], (n.mix_s, n.mix_r))
-    weight = Gather(
-        lambda slot, i: n.WO.at[at(slot, width)],
-        lambda i: n.wo,
-        (n.wo__s, n.wo__r), me, core, across,
+    dp_side = lax.rem(dp, 2)
+    weight = WeightGather(
+        n.WO, n.wo, (n.wo__s, n.wo__r), (me, core, across, dp_side, dp + 1 - 2 * dp_side)
     )
 
     def vec_copy(k):
-        return copy_to(n.vec.at[:SUBLANES], n.VEC.at[me], n.vec__s.at[k, 0], n.vec__r.at[k, 0], peers[k])
+        return copy_to(n.VIN, n.VEC.at[me], n.vec__s.at[k, 0], n.vec__r.at[k, 0], peers[k])
 
     res.start(0)
+    n.VIN[...] = jnp.zeros_like(n.VIN)
+    for row, source in enumerate((n.v1, n.v2, n.v3, n.v4)):
+        n.VIN[row : row + 1, :width] = source[...]
+    n.VIN[4:6, :width] = n.ib[...]
     for k in range(3):
         vec_copy(k).start()
     for i in range(1, blocks):
         res.start(i)
-    n.VEC[me] = n.vec[:SUBLANES]
+    n.VEC[me] = n.VIN[...]
     loads[0].wait()
     n.WN[...] = jnp.transpose(n.BM[: 3 * width])
     for ref in (n.GWE, n.GWR, n.GW, n.ACC, n.OWN, n.SQ):
@@ -405,10 +498,7 @@
     for k in range(3):
         vec_copy(k).wait_recv()
     vectors = jnp.concatenate([n.VEC[p][:, :width] for p in range(parts)], axis=1)
-    be = jnp.concatenate(
-        [n.vec[SUBLANES + p : SUBLANES + p + 1, :width] for p in range(parts)], axis=1
-    )
-    vectors = jnp.where(rows_of(vectors.shape) == 6, be, vectors)
+    vectors = jnp.where(rows_of(vectors.shape) == 6, n.be[...][None], vectors)
     vectors = jnp.concatenate([vectors, jnp.zeros((LANES - SUBLANES, D), F32)], axis=0)
     n.COLS[...] = jnp.transpose(vectors)
     loads[5].wait()
@@ -433,11 +523,6 @@
 
     def forward_block(i, _):
         res.forward(i)
-
-        @pl.when(i == 2)
-        def _():
-            weight.start(0)
-            cot.start(0)
 
         res.finish(i)
         here = tokens(i)
@@ -456,6 +541,11 @@
         live = i * SHORT < total
         allowed = diagonal(live)
         q_heads = halves(q * SCORE_SCALE)
+
+        @pl.when(i == blocks - 1)
+        def _():
+            weight.relay()
+
         carry = []
         for h in range(heads):
             s = jnp.where(allowed, dot(part_of(k_rows, h), q_heads[h]), -FAR)
@@ -486,9 +576,12 @@
             n.LSE[i, h : h + 1] = m + jnp.log(norm)
         n.MIX[own, here] = jnp.concatenate(mixed, axis=0).astype(BF16)
 
+
         @pl.when(i == 0)
         def _():
+            weight.start()
             mix.start(i)
+            cot.start(i)
 
         return 0
 
@@ -560,23 +653,20 @@
     for i in range(blocks - 1, 0, -1):
         mix.start(i)
         cot.start(i)
+    weight.forward()
     mix.forward(0)
-    weight.forward(0)
-    cot.forward(0)
-    weight.finish(0)
+    weight.finish()
     n.BM[D:] = jnp.transpose(n.WO[...])
 
     def middle_block(step, _):
         i = order(step)
         slot = lax.rem(step, 2)
 
-        @pl.when(step >= 1)
+        @pl.when(step == 1)
         def _():
             mix.forward(i)
-            cot.forward(i)
 
         mix.finish(i)
-        cot.finish(i)
         here = tokens(i)
         full, _unused = decompress(n.RES[:, here].astype(F32))
         x1 = full + center(dot(n.BM[D:], n.MIX[:, here]) + col(1))
@@ -591,6 +681,7 @@
         )
         active = active.astype(BF16)
         slope = slope.astype(BF16)
+        cot.forward(i)
 
         @pl.when(step >= 2)
         def _():
@@ -607,8 +698,14 @@
         split(slot, center(b2).astype(BF16))
         for c in b2_first(slot, i):
             c.start()
+        cot.finish(i)
         g2 = branch_grad(n.COT[:, here].astype(F32)).astype(BF16)
         n.GWR[...] += dot_nt(active, g2)
+
+        @pl.when((step >= 1) & (step < blocks - 1))
+        def _():
+            mix.forward(order(step + 1))
+
         d_hidden = (dot(n.WR[...], g2) * slope).astype(BF16)
         n.ACC[...] += dot(g2, pick(0)) + dot(d_hidden, pick(1))
         n.GWE[...] += dot_nt(rows, d_hidden)
@@ -618,12 +715,14 @@
 
     lax.fori_loop(0, blocks, middle_block, 0)
     last = (blocks - 1) % 2
+    for batch in range(2):
+        cut = slice(batch * 2 * width, (batch + 1) * 2 * width)
+        n.BM[:D, cut] = n.GWE[:, cut].astype(BF16)
+        n.BM[D:, cut] = n.GWR[:, cut].astype(BF16)
+        feeds[batch].start()
     e2_sum(order(blocks - 1))
     e2_sum(0)
     scatter_sum(n.B2C, b2_first(last, order(blocks - 1)), last, order(blocks - 1))
-    n.BM[:D] = n.GWE[...].astype(BF16)
-    n.BM[D:] = n.GWR[...].astype(BF16)
-    feed.start()
     for slot, step in ((1 - last, blocks - 2), (last, blocks - 1)):
         for c in b2_first(slot, order(step)):
             c.wait_send()
@@ -664,6 +763,22 @@
         live = lanes((1, SHORT)) + i * SHORT < total
         n.SQ[me, 0:1] += jnp.where(live, column_sum(x2 * x2), 0.0)
 
+    def service(point):
+        quarters = {1: (feed, 0), 2: (feed, 1), 3: (feed, 2), 4: (feed, 3)}
+        quarters |= {5: (feed_late, 0), 6: (feed_late, 1), 8: (feed_late, 2), 9: (feed_late, 3)}
+        owners = {9: feed, 14: feed_late}
+        thirds = {14: (feed, 0)}
+        for table, call in (
+            (quarters, lambda entry: entry[0].sum_quarter(entry[1])),
+            (owners, lambda entry: entry.sum_owners()),
+            (thirds, lambda entry: entry[0].forward(entry[1])),
+        ):
+            for when, entry in table.items():
+
+                @pl.when(point == when)
+                def _(call=call, entry=entry):
+                    call(entry)
+
     def backward_block(step, _):
         i = blocks - 1 - step
         slot = lax.rem(step, 2)
@@ -701,6 +816,7 @@
         mixed = n.MIX[own, here]
         n.GW[3 * width :] += dot_nt(mixed, g1)
         d_mixed = dot(n.WO[own], g1).astype(BF16)
+        service(5 * step)
         product = d_mixed.astype(F32) * mixed.astype(F32)
         delta = [column_sum(head_rows(product, h)) for h in range(heads)]
         lse = [n.LSE[i, h : h + 1] for h in range(heads)]
@@ -731,13 +847,7 @@
         def _():
             e2_total(i - 1)
 
-        @pl.when(step == 1)
-        def _():
-            feed.sum_quarter(2)
-
-        @pl.when(step == blocks - 1)
-        def _():
-            feed.sum_owners()
+        service(5 * step + 1)
 
         @pl.when(step >= 1)
         def _():
@@ -749,13 +859,9 @@
         def body(j, dq):
             dq = dq + pair(j, lse_far, None)
 
-            @pl.when((step == 0) & (j != 1))
+            @pl.when(j <= 1)
             def _():
-                feed.sum_quarter(lax.div(j, 2))
-
-            @pl.when((step == 1) & (j == 0))
-            def _():
-                feed.sum_quarter(3)
+                service(5 * step + 2 + j)
 
             return dq
 
@@ -784,6 +890,7 @@
             stat_copy(k, i).start()
         n.TOK[i, 0:1] = inverse
         n.TOK[i, 1:2] = full[D - 1 :]
+        service(5 * step + 4)
         return 0
 
     lax.fori_loop(0, blocks, backward_block, 0)
@@ -792,6 +899,10 @@
     n.BT[:D] = n.GW[:, : 2 * width].astype(BF16)
     n.BT[D:] = n.GW[:, 2 * width :].astype(BF16)
     rest.start()
+    feed.forward(1)
+    feed.forward(2)
+    for third in range(3):
+        feed_late.forward(third)
 
     def square_copy(k):
         return copy_to(n.SQ.at[me], n.SQ.at[me], n.sq_s.at[k, 0], n.sq_r.at[k, 0], peers[k])
@@ -809,7 +920,7 @@
         finish_grad(blocks - 1 - k)
         return 0
 
-    feed.forward()
+    rest.sum_owners()
     lax.fori_loop(0, blocks, finish_rows, 0)
     for k in range(3):
         square_copy(k).wait_recv()
@@ -850,33 +961,34 @@
     stores = [store(n.QT, n.grad, 0), store(n.VT, n.out, 1)]
     for c in stores:
         c.start()
-    rest.sum_owners()
     each_group(lambda d, group: tiny_copy(group, group).wait_recv())
     small = n.SMALL[0]
     for group in range(1, groups):
         small = small + n.SMALL[group]
     n.small[...] = small
-    feed.finish()
-
-    def store_half(target, k):
+
+    def store_batch(batch, target, k):
+        batch.finish()
+
         def body(half, rows):
             store(rows, target.at[half * D : (half + 1) * D], k + half).start()
 
-        return body
-
-    feed.take(store_half(n.feed, 2))
-    rest.forward()
-    rest.finish()
-    rest.take(store_half(n.rest, 4))
-    for k, (buf, target) in enumerate(((n.BM, n.feed), (n.BT, n.rest))):
+        batch.take(body)
         for half in range(2):
             here = slice(half * D, (half + 1) * D)
-            stores.append(store(buf.at[here], target.at[here], 2 + 2 * k + half))
+            stores.append(store(batch.buf.at[here], target.at[here], k + half))
+
+    rest.forward(0)
+    store_batch(feed, n.feed.at[:, : 2 * width], 2)
+    rest.forward(1)
+    store_batch(feed_late, n.feed.at[:, 2 * width :], 4)
+    rest.forward(2)
+    store_batch(rest, n.rest, 6)
 
     for k in range(3):
         vec_copy(k).wait_send()
         square_copy(k).wait_send()
-    weight.drain(0)
+    weight.drain()
 
     def drain(i, _):
         for g in (res, cot, mix):
@@ -893,8 +1005,8 @@
             c.wait_send()
     for c in stores:
         c.wait()
-    feed.drain()
-    rest.drain()
+    for batch in (feed, feed_late, rest):
+        batch.drain()
     each_group(lambda d, group: tiny_copy(dp, group).wait_send())
 
 
@@ -911,24 +1023,25 @@
     gwe_ref[...] = feed_low[...].astype(F32)
     gwr_ref[...] = feed_high[...].astype(F32)
 
-    @pl.when(i < 3)
+    most = pl.num_programs(0) * 3 // 4
+
+    @pl.when(i < most)
     def _():
         gw_ref[...] = rest
 
-    @pl.when(i == 3)
+    @pl.when(i >= most)
     def _():
         gwo_ref[...] = rest
 
     @pl.when(i == 0)
     def _():
         gb_ref[...] = small[0:2, :width]
-        gg_one_ref[...] = small[2:3, :width]
-        gbo_ref[...] = small[4:5, :width]
-        gg_two_ref[...] = small[5:6, :width]
-        gbr_ref[...] = small[6:7, :width]
-        gbe_ref[...] = jnp.concatenate(
-            [small[8 + p : 9 + p, :width] for p in range(D // width)], axis=1
-        )
+        gg_one_ref[...] = small[2, :width]
+        gbo_ref[...] = small[4, :width]
+        gg_two_ref[...] = small[5, :width]
+        gbr_ref[...] = small[6, :width]
+        for p in range(D // width):
+            gbe_ref[p * width : (p + 1) * width] = small[8 + p, :width]
         live = small[7:8, 0:1]
         rms_ref[...] = jnp.sqrt(small[3:4, 0:1] / (D * live))
         live_ref[...] = live.astype(jnp.int32)
@@ -956,12 +1069,6 @@
     def shape(*dims, dtype=F32):
         return jax.ShapeDtypeStruct(dims, dtype)
 
-    zero = jnp.zeros((2, width), F32)
-    vec = jnp.concatenate(
-        [gain_one[None], output_bias[None], gain_two[None], reduce_bias[None], input_bias, zero]
-        + [expand_bias.reshape(parts, width), zero, zero]
-    )
-    vec = jnp.pad(vec, ((0, 0), (0, 2 * LANES - width)))
     groups = lax.axis_size("dp")
     names, scratches = scratch(count, width, hidden, groups)
 
@@ -988,7 +1095,12 @@
         lengths,
         residual.T,
         cotangent.T,
-        vec,
+        gain_one[None],
+        output_bias[None],
+        gain_two[None],
+        reduce_bias[None],
+        input_bias,
+        expand_bias,
         jnp.transpose(input_weight, (0, 2, 1)).reshape(3 * width, D),
         output_weight,
         expand_weight,
@@ -1004,33 +1116,34 @@
     def clip(high, wide, first, last):
         return pl.BlockSpec((high, wide), lambda i: (jnp.clip(i - first, 0, last - first), 0))
 
-    step = D // parts
-    thin = width // parts
+    steps = parts
+    step = D // steps
+    thin = width // steps
     out, grad, gw, gwo, gwe, gwr, *vectors = pl.pallas_call(
         finish_kernel,
-        grid=(parts,),
+        grid=(steps,),
         in_specs=[
             rows(thin, count),
             rows(thin, count),
             rows(step, 2 * width),
-            rows(step, 2 * width, parts),
+            rows(step, 2 * width, steps),
             rows(step, hidden),
-            rows(step, hidden, parts),
+            rows(step, hidden, steps),
             whole(16, 2 * LANES),
         ],
         out_specs=[
             rows(thin, count),
             rows(thin, count),
-            clip(width, D, 0, 2),
-            clip(width, D, 3, 3),
+            clip(step, D, 0, steps * 3 // 4 - 1),
+            clip(step, D, steps * 3 // 4, steps - 1),
             rows(step, hidden),
             rows(step, hidden),
             whole(2, width),
-            whole(1, width),
-            whole(1, width),
-            whole(1, width),
-            whole(1, hidden),
-            whole(1, width),
+            whole(width),
+            whole(width),
+            whole(width),
+            whole(hidden),
+            whole(width),
             whole(1, 1),
             whole(1, 1),
         ],
@@ -1042,11 +1155,11 @@
             shape(D, hidden),
             shape(hidden, D),
             shape(2, width),
-            shape(1, width),
-            shape(1, width),
-            shape(1, width),
-            shape(1, hidden),
-            shape(1, width),
+            shape(width),
+            shape(width),
+            shape(width),
+            shape(hidden),
+            shape(width),
             shape(1, 1),
             shape(1, 1, dtype=jnp.int32),
         ],
@@ -1060,13 +1173,13 @@
         jnp.transpose(gw.reshape(3, width, D), (0, 2, 1)),
         gb,
         gwo,
-        gbo[0],
-        gg_one[0],
-        gg_two[0],
+        gbo,
+        gg_one,
+        gg_two,
         gwe,
-        gbe[0],
+        gbe,
         gwr,
-        gbr[0],
+        gbr,
         rms[0, 0],
         live_count[0, 0],
     )

time: 201 us -> 187 us (0.930)
  Pallas kernels: 196 us -> 186 us
  local copies, waits for them, and re-layouts: 2.17 us -> 0 us
    pallas_call x1, Pallas kernels: 189 us -> 180 us  [on_device(): pl.pallas_call(lambda *refs: layer_kernel(groups, names, *refs), in_specs...]
where the time goes in v4:
time: 187 us
  Pallas kernels  186 us (99%)
    pallas_call x1, Pallas kernels, on_device(): pl.pallas_call(lambda *refs: layer_kernel(groups, names, *refs), in_specs...  180 us
    pallas_call x1, Pallas kernels, on_device(): pl.pallas_call(finish_kernel, grid=(steps,), in_specs=[rows(thin, count),...  6.65 us

profile of v4, /device:TPU:0, one launch (start us, length us, event | category | flops | bytes accessed | tf_op | source)
XLA Modules:
  0.0 187.0 jit_solution(7996976370905167737)
XLA Ops:
  0.7 179.5 %layer.1 = (bf16[192,2048]{1,0:T(8,128)(2,1)}, bf16[192,2048]{1,0:T(8,128)(2,1)}, bf16[1536,384]{1,0:T(8,128)(2,1)}, bf16[1536,768]{1,0:T(8,128)(2,1)}, f32[16,256]{1,0:T(8,128)}) custom-call(s32[1,4]{1,0:T(1,128)} %refs_0_.1, bf16[192,2048]{1,0:T(8,128)(2,1)} %bitcast.17, bf16[192,2048]{1,0:T(8,128)(2,1)} %bitcast.18, f32[1,192]{1,0:T(1,128)} %bitcast.19, ...), custom_call_target="tpu_custom_call" | custom-call | tf_op jit(solution)/shard_map/layer/pallas_call | solution.py:1078
  180.2 6.7 %finish.1 = (bf16[192,2048]{1,0:T(8,128)(2,1)}, bf16[192,2048]{1,0:T(8,128)(2,1)}, f32[576,768]{1,0:T(8,128)}, f32[192,768]{1,0:T(8,128)}, f32[768,768]{1,0:T(8,...) custom-call(bf16[192,2048]{1,0:T(8,128)(2,1)} %get-tuple-element.33., ...), custom_call_target="tpu_custom_call" | custom-call | tf_op jit(solution)/shard_map/finish/pallas_call | solution.py:1122

commit v5 on v4

--- a/solution.py
+++ b/solution.py
@@ -920,7 +920,6 @@
         finish_grad(blocks - 1 - k)
         return 0
 
-    rest.sum_owners()
     lax.fori_loop(0, blocks, finish_rows, 0)
     for k in range(3):
         square_copy(k).wait_recv()
@@ -954,6 +953,7 @@
     table = jnp.concatenate([table, jnp.zeros((2 * LANES - width, LANES), F32)], axis=0)
     n.SMALL[dp] = jnp.transpose(table)[:16]
     each_group(lambda d, group: tiny_copy(dp, group).start())
+    rest.sum_owners()
 
     def store(src, dst, k):
         return pltpu.make_async_copy(src, dst, n.store_s.at[0, k])

time: 187 us -> 184 us (0.984)
  Pallas kernels: 186 us -> 183 us
    pallas_call x1, Pallas kernels: 180 us -> 177 us  [on_device(): pl.pallas_call(lambda *refs: layer_kernel(groups, names, *refs), in_specs...]
where the time goes in v5:
time: 184 us
  Pallas kernels  183 us (99%)
    pallas_call x1, Pallas kernels, on_device(): pl.pallas_call(lambda *refs: layer_kernel(groups, names, *refs), in_specs...  177 us
    pallas_call x1, Pallas kernels, on_device(): pl.pallas_call(finish_kernel, grid=(steps,), in_specs=[rows(thin, count),...  6.65 us

profile of v5, /device:TPU:0, one launch (start us, length us, event | category | flops | bytes accessed | tf_op | source)
XLA Modules:
  0.0 184.0 jit_solution(8383133014953079346)
XLA Ops:
  0.7 176.6 %layer.1 = (bf16[192,2048]{1,0:T(8,128)(2,1)}, bf16[192,2048]{1,0:T(8,128)(2,1)}, bf16[1536,384]{1,0:T(8,128)(2,1)}, bf16[1536,768]{1,0:T(8,128)(2,1)}, f32[16,256]{1,0:T(8,128)}) custom-call(s32[1,4]{1,0:T(1,128)} %refs_0_.1, bf16[192,2048]{1,0:T(8,128)(2,1)} %bitcast.17, bf16[192,2048]{1,0:T(8,128)(2,1)} %bitcast.18, f32[1,192]{1,0:T(1,128)} %bitcast.19, ...), custom_call_target="tpu_custom_call" | custom-call | tf_op jit(solution)/shard_map/layer/pallas_call | solution.py:1078
  177.2 6.7 %finish.1 = (bf16[192,2048]{1,0:T(8,128)(2,1)}, bf16[192,2048]{1,0:T(8,128)(2,1)}, f32[576,768]{1,0:T(8,128)}, f32[192,768]{1,0:T(8,128)}, f32[768,768]{1,0:T(8,...) custom-call(bf16[192,2048]{1,0:T(8,128)(2,1)} %get-tuple-element.33., ...), custom_call_target="tpu_custom_call" | custom-call | tf_op jit(solution)/shard_map/finish/pallas_call | solution.py:1122
